TPU v7x, 1024 devices: a whole 4x8x16 slice. The times are simulated.
1024 devices in a mesh: ctx: 16 (over z), chan: 64 (over x, y, core).
Axes of the slice: x: 4, y: 8, z: 16, core: 2. Of those that a mesh axis runs over, the one named last changes fastest.
Arguments:
- query: bfloat16 [8192, 8192], P('ctx', 'chan'), may hold values from -6 to 6
- key_in: bfloat16 [8192, 8192], P('ctx', 'chan'), may hold values from -6 to 6
- value: bfloat16 [8192, 8192], P('ctx', 'chan'), may hold values from -11 to 11
- decay: float32 [512, 16], P('chan'), may hold values from 1.2207031e-05 to 0.0333333333, as said below
- residue: float32 [512, 16], P('chan'), may hold values from -0.2 to 0.2
- skip: float32 [8192], P('chan'), may hold values from -4 to 4
- norm_gain: float32 [8192], P('chan'), may hold values from 0.1 to 1.9
Outputs:
- mixed: bfloat16 [8192, 8192], P('ctx', 'chan')
Inputs may be any that keep to these rules, and one draw needn't show every extreme that they name: `decay`: rates differ from filter to filter and mode to mode.
All inputs are finite; a program needn't handle non-finite values.
Results may differ from a plain program's by a relative error of at most 0.0015.
Values sent between devices are 32-bit elements; how exact they have to be, the bound alone decides.
No kernel may reach another device: no remote copies, remote signals or barrier semaphores. Data moves between devices by JAX's collectives and lax.ppermute only.
A program may use at most 32 MiB of HBM per device.

v0:
```python
import jax
import jax.numpy as jnp
from jax import lax
from jax.sharding import PartitionSpec as P

D = 8192


def whole_conv(signal, rate_piece, res_piece, block):
    highest = lax.Precision.HIGHEST
    pieces, per_group, length = signal.shape
    count = length // block
    positions = jnp.arange(block, dtype=jnp.float32)
    left_modes = res_piece[:, None, :] * jnp.exp(-rate_piece[:, None, :] * positions[None, :, None])
    right_modes = jnp.exp(rate_piece[:, None, :] * positions[None, :, None])
    toeplitz = jnp.einsum("gtm,gsm->gts", left_modes, right_modes, precision=highest)
    causal = positions[:, None] >= positions[None, :]
    toeplitz = jnp.where(causal[None, :, :], toeplitz, 0.0)
    blocks = signal.reshape(pieces, per_group, count, block)
    near_part = jnp.einsum("gts,gcks->gckt", toeplitz, blocks, precision=highest)
    end_powers = jnp.exp(-rate_piece[:, None, :] * (block - 1.0 - positions)[None, :, None])
    own_end = jnp.einsum("gsm,gcks->gckm", end_powers, blocks, precision=highest)
    block_index = jnp.arange(count, dtype=jnp.float32)
    distance = jnp.maximum(block_index[:, None] - 1.0 - block_index[None, :], 0.0)
    earlier = block_index[None, :] < block_index[:, None]
    factors = jnp.exp(-rate_piece[:, :, None, None] * block * distance[None, None, :, :])
    factors = jnp.where(earlier[None, None, :, :], factors, 0.0)
    incoming = jnp.einsum("gmkj,gcjm->gckm", factors, own_end, precision=highest)
    far_modes = res_piece[:, None, :] * jnp.exp(
        -rate_piece[:, None, :] * (positions + 1.0)[None, :, None]
    )
    far_part = jnp.einsum("gtm,gckm->gckt", far_modes, incoming, precision=highest)
    return (near_part + far_part).reshape(pieces, per_group, length)


def local(query, key_in, value, decay, residue, skip, norm_gain):
    tok_rows, chan_width = query.shape
    groups, mode_count = decay.shape
    group_width = chan_width // groups
    gated = query.astype(jnp.float32) * key_in.astype(jnp.float32)
    ctx_count = lax.axis_size("ctx")
    share = chan_width // ctx_count
    length = tok_rows * ctx_count
    block = min(length, max(512, tok_rows))
    outgoing = jnp.transpose(gated).reshape(ctx_count, share, tok_rows)
    mine = lax.all_to_all(outgoing, "ctx", split_axis=0, concat_axis=2, tiled=True)
    pieces = max(1, share // group_width)
    per_group = share // pieces
    first_group = lax.axis_index("ctx") * share // group_width
    rate_piece = lax.dynamic_slice_in_dim(decay, first_group, pieces, 0)
    res_piece = lax.dynamic_slice_in_dim(residue, first_group, pieces, 0)
    convolved = whole_conv(mine, rate_piece, res_piece, block)
    returned = lax.all_to_all(convolved, "ctx", split_axis=2, concat_axis=0, tiled=True)
    conv_total = jnp.transpose(returned.reshape(chan_width, tok_rows))
    out_gate = value.astype(jnp.float32) * (conv_total + skip[None, :] * gated)
    local_squares = jnp.sum(out_gate * out_gate, axis=1)
    total_squares = lax.psum(local_squares, "chan")
    scale = lax.rsqrt(total_squares / D + 1e-05)
    mixed = out_gate * norm_gain[None, :] * scale[:, None]
    return mixed.astype(jnp.bfloat16)


def solution(mesh):
    placed = (
        P("ctx", "chan"),
        P("ctx", "chan"),
        P("ctx", "chan"),
        P("chan", None),
        P("chan", None),
        P("chan"),
        P("chan"),
    )
    return jax.shard_map(
        local, mesh=mesh, in_specs=placed, out_specs=P("ctx", "chan"), check_vma=False
    )
```

profile of v0, /device:TPU:1, one launch (start us, length us, event | category | flops | bytes accessed | tf_op | source)
XLA Modules:
  0.0 252.2 jit_solution(4053635907591753615)
XLA Ops:
  0.0 0.0 copy-start
  0.0 1.0 copy.25
  1.0 1.0 copy.26
  2.0 0.7 fusion.9
  2.8 19.4 %all-to-all-start = ((f32[16,8,512]{2,1,0:T(8,128)}), f32[16,8,512]{2,1,0:T(8,128)S(1)}, u32[]{:S(2)}, u32[]{:S(2)}) async-start(f32[16,8,512]{2,1,0:T(8,128)} %fusion.9), calls=%async_computation | async-start | bytes 524288 | tf_op jit(solution)/shard_map/all_to_all | solution.py:46
  22.2 0.7 broadcast_multiply_fusion
  22.9 0.0 copy-done
  23.0 1.1 fusion
  24.1 0.1 subtract_maximum_fusion
  24.2 11.1 %all-to-all-done = f32[16,8,512]{2,1,0:T(8,128)S(1)} async-done(((f32[16,8,512]{2,1,0:T(8,128)}), f32[16,8,512]{2,1,0:T(8,128)S(1)}, u32[]{:S(2)}, u32[]{:S(2)}) %all-to-all-start) | async-done | bytes 262176 | tf_op jit(solution)/shard_map/all_to_all | solution.py:46
  35.3 0.5 fusion.2
  35.8 0.1 copy.28
  35.9 0.4 convolution_bitcast_fusion
  36.3 1.3 fusion.4
  37.6 0.4 convolution_add_fusion
  38.0 2.6 %copy.34 = f32[8,16,512]{0,2,1:T(8,128)} copy(f32[8,16,512]{2,1,0:T(8,128)S(1)} %convolution_add_fusion) | data formatting | bytes 524288 | tf_op jit(solution)/shard_map/reshape | solution.py:33
  40.7 0.5 broadcast.121
  41.2 38.4 %reduce = f32[8192,8]{1,0:T(8,128)} reduce(f32[8192,1,8]{2,1,0:T(1,128)} %bitcast.49, f32[]{:T(128)} %broadcast.121), dimensions={1}, to_apply=%bitcast.44.reduce_sub_computation | reduce | bytes 524292
  79.5 0.0 copy-start.1
  79.5 4.4 %reshape.221 = f32[16,1,4096]{2,1,0:T(1,128)} reshape(f32[8192,8]{1,0:T(8,128)} %reduce) | data formatting | bytes 524288
  84.0 11.0 %all-to-all-start.1 = ((f32[16,1,4096]{2,1,0:T(1,128)}), f32[16,1,4096]{2,1,0:T(1,128)S(1)}, u32[]{:S(2)}, u32[]{:S(2)}) async-start(f32[16,1,4096]{2,1,0:T(1,128)} %reshape.221), calls=%async_computation.1 | async-start | bytes 524288 | tf_op jit(solution)/shard_map/all_to_all | solution.py:53
  95.0 0.0 copy-done.1
  95.0 0.1 copy.24
  95.1 12.9 %all-to-all-done.1 = f32[16,1,4096]{2,1,0:T(1,128)S(1)} async-done(((f32[16,1,4096]{2,1,0:T(1,128)}), f32[16,1,4096]{2,1,0:T(1,128)S(1)}, u32[]{:S(2)}, u32[]{:S(2)}) %all-to-all-start.1) | async-done | bytes 262176 | tf_op jit(solution)/shard_map/all_to_all | solution.py:53
  108.0 1.3 reduce.1
  109.3 0.0 copy-start.2
  109.3 0.0 copy-start.3
  109.3 8.4 %reshape.222 = f32[8192,1,8]{2,1,0:T(1,128)} reshape(f32[16,4096]{1,0:T(8,128)S(1)} %reduce.1) | data formatting | bytes 524288
  117.7 2.8 %copy.35 = f32[1,8,16,512]{3,2,1,0:T(8,128)S(1)} copy(f32[1,8,16,512]{1,3,2,0:T(8,128)} %bitcast.50) | data formatting | bytes 524288 | tf_op jit(solution)/shard_map/all_to_all | solution.py:53
  120.5 0.0 copy-done.2
  120.5 0.2 multiply_reduce_fusion
  120.7 130.5 %psum.7 = f32[512]{0:T(512)S(1)} all-reduce(f32[512]{0:T(512)S(1)} %multiply_reduce_fusion), channel_id=1, replica_groups=mesh['ctx'=16,'chan'=64] {'chan'}, use_global_device_ids=true, to_apply=%region_1.2 | all-reduce | flops 512 | bytes 4096 | tf_op jit(solution)/shard_map/psum | solution.py:57
  251.2 0.0 copy-done.3
  251.2 0.2 multiply_convert_fusion
  251.5 0.8 copy.33
  (7 shorter events, 0.1 us)
Async XLA Ops:
  0.0 22.9 %copy-start = (f32[8,16]{1,0:T(8,128)S(1)}, f32[8,16]{1,0:T(8,128)}, u32[]{:S(2)}) copy-start(f32[8,16]{1,0:T(8,128)} %param.11) | copy-start | bytes 1540
  2.8 32.6 %all-to-all-start = ((f32[16,8,512]{2,1,0:T(8,128)}), f32[16,8,512]{2,1,0:T(8,128)S(1)}, u32[]{:S(2)}, u32[]{:S(2)}) async-start(f32[16,8,512]{2,1,0:T(8,128)} %fusion.9), calls=%async_computation | async-start | bytes 524288 | tf_op jit(solution)/shard_map/all_to_all | solution.py:46
  79.5 15.4 %copy-start.1 = (bf16[512,128]{1,0:T(8,128)(2,1)S(1)}, bf16[512,128]{1,0:T(8,128)(2,1)}, u32[]{:S(2)}) copy-start(bf16[512,128]{1,0:T(8,128)(2,1)} %param.9) | copy-start | bytes 393220
  84.0 24.0 %all-to-all-start.1 = ((f32[16,1,4096]{2,1,0:T(1,128)}), f32[16,1,4096]{2,1,0:T(1,128)S(1)}, u32[]{:S(2)}, u32[]{:S(2)}) async-start(f32[16,1,4096]{2,1,0:T(1,128)} %reshape.221), calls=%async_computation.1 | async-start | bytes 524288 | tf_op jit(solution)/shard_map/all_to_all | solution.py:53
  109.3 11.2 %copy-start.2 = (f32[128]{0:T(128)S(1)}, f32[128]{0:T(128)}, u32[]{:S(2)}) copy-start(f32[128]{0:T(128)} %param.12) | copy-start | bytes 1540
  109.3 141.9 %copy-start.3 = (f32[128]{0:T(128)S(1)}, f32[128]{0:T(128)}, u32[]{:S(2)}) copy-start(f32[128]{0:T(128)} %param.13) | copy-start | bytes 1540
where the time goes:
time: 254 us; the launch traced here: 252 us
  blocking collectives  130 us (51%)
  other arithmetic  41.6 us (16%)
  starting transfers between devices  30.4 us (12%)
  waiting for transfers between devices  24.1 us (9%)
  local copies, waits for them, and re-layouts  21.8 us (9%)
  matrix products  3.71 us (1%)
    psum x1, blocking collectives, local(): total_squares = lax.psum(local_squares, 'chan')  130 us
    unnamed x1, other arithmetic  38.4 us
    all_to_all x1, starting transfers between devices, local(): lax.all_to_all(outgoing, 'ctx', split_axis=0, concat_axis=2, tiled=True)  19.4 us
    unnamed x14, local copies, waits for them, and re-layouts  15.5 us
    all_to_all x1, waiting for transfers between devices, local(): lax.all_to_all(convolved, 'ctx', split_axis=2, concat_axis=0, tiled=True)  12.9 us
    all_to_all x1, waiting for transfers between devices, local(): lax.all_to_all(outgoing, 'ctx', split_axis=0, concat_axis=2, tiled=True)  11.1 us
    all_to_all x1, starting transfers between devices, local(): lax.all_to_all(convolved, 'ctx', split_axis=2, concat_axis=0, tiled=True)  11 us
  transfers between devices with their start and end apart: 2, of which 2 were waited for; matrix products, arithmetic and copies ran while one was open for 1% of the time, Pallas kernels for 0%

commit v1 on v0

v1 whole, which is shorter than its diff:
```python
import jax
import jax.numpy as jnp
from jax import lax
from jax.experimental import pallas as pl
from jax.experimental.pallas import tpu as pltpu
from jax.sharding import PartitionSpec as P

D = 8192
EPS = 1e-05
CHUNK = 128
F32 = jnp.float32
BF16 = jnp.bfloat16
VMEM_BYTES = 24 << 20


def iota(shape, dim):
    return lax.broadcasted_iota(jnp.int32, shape, dim)


def split(x):
    high = x.astype(BF16)
    low = (x - high.astype(F32)).astype(BF16)
    return high, low


def dot(a, b):
    return jnp.dot(a, b, preferred_element_type=F32)


def wide_lhs(x):
    return jnp.concatenate(split(x), axis=1)


def wide_dot(lhs, x):
    pair = jnp.concatenate(split(x), axis=1)
    both = dot(lhs, jnp.concatenate([pair, pair], axis=0))
    width = x.shape[1]
    return both[:, :width] + both[:, width:]


def mode_column(table):
    groups, modes = table.shape
    rows = groups * modes
    spread = jnp.broadcast_to(table[:, None, :], (groups, modes, modes)).reshape(rows, modes)
    own = iota((rows, modes), 0) % modes == iota((rows, modes), 1)
    return jnp.sum(jnp.where(own, spread, 0.0), axis=1, keepdims=True)


def to_row(column):
    n = column.shape[0]
    diagonal = iota((n, n), 0) == iota((n, n), 1)
    return jnp.sum(jnp.where(diagonal, jnp.broadcast_to(column, (n, n)), 0.0), axis=0, keepdims=True)


def own_group(modes, width, per_group):
    rows = width // per_group * modes
    return iota((rows, width), 0) // modes == iota((rows, width), 1) // per_group


def fold(full, groups):
    rows, width = full.shape
    return jnp.sum(full.reshape(groups, rows // groups, width), axis=0)


def end_kernel(query_ref, key_ref, decay_ref, send_ref):
    tokens, width = query_ref.shape
    groups, modes = decay_ref.shape
    targets = send_ref.shape[0]
    me = lax.axis_index("ctx")
    rate = mode_column(decay_ref[...])
    mask = own_group(modes, width, width // groups)
    age = (tokens - 1 - iota((groups * modes, tokens), 1)).astype(F32)
    lhs = split(jnp.exp(-rate * age))
    gated = query_ref[...].astype(F32) * key_ref[...].astype(F32)
    high, low = split(gated)
    full = dot(lhs[0], high) + (dot(lhs[1], high) + dot(lhs[0], low))
    state = fold(jnp.where(mask, full, 0.0), groups)
    block_rate = fold(jnp.where(mask, rate * float(tokens), 0.0), groups)
    for target in range(targets):
        between = target - 1 - me
        decayed = state * jnp.exp(-block_rate * jnp.maximum(between, 0).astype(F32))
        send_ref[target] = jnp.where(between >= 0, decayed, 0.0)


def near_kernel(query_ref, key_ref, decay_ref, residue_ref, skip_ref, near_ref, far_ref):
    tokens, width = query_ref.shape
    groups, modes = decay_ref.shape
    per_group = width // groups
    rows = groups * modes
    decay, residue = decay_ref[...], residue_ref[...]
    rate = mode_column(decay)
    rate_row, residue_row = to_row(rate), to_row(mode_column(residue))
    since = (iota((tokens, rows), 0) + 1).astype(F32)
    far = wide_lhs(residue_row * jnp.exp(-rate_row * since))
    far_ref[...] = far
    lag = ((CHUNK - iota((groups, CHUNK), 1)) % CHUNK).astype(F32)
    taps = jnp.zeros((groups, CHUNK), F32)
    for m in range(modes):
        taps += residue[:, m : m + 1] * jnp.exp(-decay[:, m : m + 1] * lag)
    causal = iota((CHUNK, CHUNK), 0) >= iota((CHUNK, CHUNK), 1)
    left = []
    for g in range(groups):
        spread = jnp.broadcast_to(taps[g : g + 1], (CHUNK, CHUNK))
        turned = pltpu.roll(spread, 0, 1, stride=1, stride_axis=0)
        left.append(wide_lhs(jnp.where(causal, turned, 0.0)))
    age = (CHUNK - 1 - iota((rows, CHUNK), 1)).astype(F32)
    ends = wide_lhs(jnp.exp(-rate * age))
    step = jnp.exp(-rate * float(CHUNK))
    mask = own_group(modes, width, per_group)
    lane_group = iota((CHUNK, width), 1) // per_group
    skip = skip_ref[...]
    state = None
    for i in range(tokens // CHUNK):
        part = pl.ds(i * CHUNK, CHUNK)
        gated = query_ref[part, :].astype(F32) * key_ref[part, :].astype(F32)
        out = skip * gated
        pair = jnp.concatenate(split(gated), axis=1)
        right = jnp.concatenate([pair, pair], axis=0)
        conv = jnp.zeros((CHUNK, width), F32)
        for g in range(groups):
            both = dot(left[g], right)
            conv = jnp.where(lane_group == g, both[:, :width] + both[:, width:], conv)
        out += conv
        if state is not None:
            out += wide_dot(far[:CHUNK], state)
        near_ref[part, :] = out
        if (i + 1) * CHUNK < tokens:
            both = dot(ends, right)
            end = jnp.where(mask, both[:, :width] + both[:, width:], 0.0)
            state = end if state is None else step * state + end


def gate_kernel(got_ref, near_ref, far_ref, value_ref, out_ref, send_ref):
    tokens, width = near_ref.shape
    modes = got_ref.shape[1]
    rows = far_ref.shape[1] // 2
    groups = rows // modes
    state = got_ref[0]
    for source in range(1, got_ref.shape[0]):
        state += got_ref[source]
    mask = own_group(modes, width, width // groups)
    tiled = jnp.concatenate([state] * groups, axis=0)
    full = jnp.where(mask, tiled, 0.0)
    out = value_ref[...].astype(F32) * (near_ref[...] + wide_dot(far_ref[...], full))
    out_ref[...] = out
    squares = out * out
    sums = []
    for i in range(tokens // CHUNK):
        turned = jnp.transpose(squares[i * CHUNK : (i + 1) * CHUNK])
        sums.append(jnp.sum(turned, axis=0, keepdims=True))
    sums = jnp.concatenate(sums, axis=0)
    send_ref[...] = jnp.broadcast_to(sums[None], send_ref.shape)


def norm_kernel(got_ref, out_ref, gain_ref, mixed_ref):
    width = out_ref.shape[1]
    total = jnp.sum(got_ref[...], axis=0)
    scale = lax.rsqrt(total / D + EPS)
    for i in range(scale.shape[0]):
        part = pl.ds(i * CHUNK, CHUNK)
        column = jnp.transpose(jnp.broadcast_to(scale[i : i + 1], (width, CHUNK)))
        mixed_ref[part, :] = (out_ref[part, :] * gain_ref[...] * column).astype(BF16)


def call(kernel, outs, flops, size):
    return pl.pallas_call(
        kernel,
        out_shape=outs,
        compiler_params=pltpu.CompilerParams(vmem_limit_bytes=VMEM_BYTES),
        cost_estimate=pl.CostEstimate(flops=flops, bytes_accessed=size, transcendentals=0),
    )


def local(query, key_in, value, decay, residue, skip, norm_gain):
    tokens, width = query.shape
    groups, modes = decay.shape
    ctx, chan = lax.axis_size("ctx"), lax.axis_size("chan")
    shape = jax.ShapeDtypeStruct
    with jax.named_scope("end_state"):
        send = call(end_kernel, shape((ctx, modes, width), F32), 10**8, 10**6)(query, key_in, decay)
    with jax.named_scope("exchange_states"):
        got = lax.all_to_all(send, "ctx", 0, 0)
    with jax.named_scope("near_conv"):
        near, far = call(
            near_kernel,
            (shape((tokens, width), F32), shape((tokens, 2 * groups * modes), BF16)),
            10**9,
            4 * 10**6,
        )(query, key_in, decay, residue, skip[None, :])
    with jax.named_scope("gate"):
        out, send = call(
            gate_kernel,
            (shape((tokens, width), F32), shape((chan, tokens // CHUNK, CHUNK), F32)),
            10**8,
            10**6,
        )(got, near, far, value)
    with jax.named_scope("exchange_squares"):
        got = lax.all_to_all(send, "chan", 0, 0)
    with jax.named_scope("normalize"):
        return call(norm_kernel, shape((tokens, width), BF16), 10**6, 10**6)(
            got, out, norm_gain[None, :]
        )


def solution(mesh):
    placed = (
        P("ctx", "chan"),
        P("ctx", "chan"),
        P("ctx", "chan"),
        P("chan", None),
        P("chan", None),
        P("chan"),
        P("chan"),
    )
    return jax.shard_map(
        local, mesh=mesh, in_specs=placed, out_specs=P("ctx", "chan"), check_vma=False
    )
```

time: 254 us -> 61.2 us (0.24)
  blocking collectives: 130 us -> 23.9 us
  other arithmetic: 41.6 us -> 0 us
  local copies, waits for them, and re-layouts: 21.8 us -> 3.78 us
  waiting for transfers between devices: 24.1 us -> 10.1 us
  starting transfers between devices: 30.4 us -> 19.5 us
  matrix products: 3.71 us -> 0 us
  Pallas kernels: 0 us -> 3.48 us
    psum x1 -> x0, blocking collectives: 130 us -> none  [local(): total_squares = lax.psum(local_squares, 'chan')]
    unnamed x1 -> x0, other arithmetic: 38.4 us -> none
    all_to_all x0 -> x1, blocking collectives: none -> 23.9 us  [local(): got = lax.all_to_all(send, 'chan', 0, 0)]
    all_to_all x2 -> x1, waiting for transfers between devices: 24.1 us -> 10.1 us  [local(): got = lax.all_to_all(send, 'ctx', 0, 0)]
    unnamed x14 -> x20, local copies, waits for them, and re-layouts: 15.5 us -> 3.78 us
    all_to_all x2 -> x1, starting transfers between devices: 30.4 us -> 19.5 us  [local(): got = lax.all_to_all(send, 'ctx', 0, 0)]
    dot_general x5 -> x0, matrix products: 3.71 us -> none  [the longest x1 1.28 us: whole_conv(): jnp.einsum('gts,gcks->gckt', toeplitz, blocks, precision=highest)]
    pallas_call x0 -> x4, Pallas kernels: none -> 3.48 us  [the longest x1 1.24 us: local(): call(near_kernel, (shape((tokens, width), F32), shape((tokens, 2 * groups...]
  transfers between devices with their start and end apart: 2 -> 1, of which waited for: 2 -> 1; matrix products, arithmetic and copies ran while one was open for 1% -> 0% of each run, Pallas kernels for 0% -> 2%
where the time goes in v1:
time: 61.2 us; the launch traced here: 60.9 us
  blocking collectives  23.9 us (39%)
  starting transfers between devices  19.5 us (32%)
  waiting for transfers between devices  10.1 us (17%)
  local copies, waits for them, and re-layouts  3.78 us (6%)
  Pallas kernels  3.48 us (6%)
    all_to_all x1, blocking collectives, local(): got = lax.all_to_all(send, 'chan', 0, 0)  23.9 us
    all_to_all x1, starting transfers between devices, local(): got = lax.all_to_all(send, 'ctx', 0, 0)  19.5 us
    all_to_all x1, waiting for transfers between devices, local(): got = lax.all_to_all(send, 'ctx', 0, 0)  10.1 us
    unnamed x20, local copies, waits for them, and re-layouts  3.78 us
    pallas_call x1, Pallas kernels, local(): call(near_kernel, (shape((tokens, width), F32), shape((tokens, 2 * groups...  1.24 us
  transfers between devices with their start and end apart: 1, of which 1 were waited for; matrix products, arithmetic and copies ran while one was open for 0% of the time, Pallas kernels for 2%

profile of v1, /device:TPU:1, one launch (start us, length us, event | category | flops | bytes accessed | tf_op | source)
XLA Modules:
  0.0 60.9 jit_solution(13752961900335313777)
XLA Ops:
  0.0 0.0 copy-start
  0.0 0.9 %copy-done = bf16[512,128]{1,0:T(8,128)(2,1)S(1)} copy-done((bf16[512,128]{1,0:T(8,128)(2,1)S(1)}, bf16[512,128]{1,0:T(8,128)(2,1)}, u32[]{:S(2)}) %copy-start) | copy-done | bytes 131096
  0.9 0.0 copy-start.2
  0.9 0.9 %copy-done.2 = bf16[512,128]{1,0:T(8,128)(2,1)S(1)} copy-done((bf16[512,128]{1,0:T(8,128)(2,1)S(1)}, bf16[512,128]{1,0:T(8,128)(2,1)}, u32[]{:S(2)}) %copy-start.2) | copy-done | bytes 131096
  1.8 0.0 copy-start.5
  1.8 0.7 %copy-done.5 = f32[8,16]{1,0:T(8,128)S(1)} copy-done((f32[8,16]{1,0:T(8,128)S(1)}, f32[8,16]{1,0:T(8,128)}, u32[]{:S(2)}) %copy-start.5) | copy-done | bytes 536
  2.5 0.0 copy-start.6
  2.5 0.0 copy-start.8
  2.5 1.0 %end_state.1 = f32[16,16,128]{2,1,0:T(8,128)} custom-call(bf16[512,128]{1,0:T(8,128)(2,1)S(1)} %copy-done, bf16[512,128]{1,0:T(8,128)(2,1)S(1)} %copy-done.2, f32[8,16]{1,0:T(8,128)S(1)} %copy-done.5), custom_call_target="tpu_custom_call" | custom-call | flops 100000000 | bytes 1000000 | tf_op jit(solution)/shard_map/end_state/pallas_call | solution.py:180
  3.5 0.0 copy-start.1
  3.5 0.0 copy-start.3
  3.5 19.5 %all-to-all-start = ((f32[16,16,128]{2,1,0:T(8,128)}), f32[16,16,128]{2,1,0:T(8,128)S(1)}, u32[]{:S(2)}, u32[]{:S(2)}) async-start(f32[16,16,128]{2,1,0:T(8,128)} %end_state.1), calls=%async_computation | async-start | bytes 262144 | tf_op jit(solution)/shard_map/exchange_states/all_to_all | solution.py:182
  23.1 0.0 copy-start.9
  23.1 0.0 copy-done.6
  23.1 0.0 copy-done.8
  23.1 0.0 copy-done.1
  23.1 0.0 copy-done.3
  23.1 0.6 copy-done.9
  23.7 0.0 copy-start.4
  23.7 1.2 %near_conv.1 = (f32[512,128]{1,0:T(8,128)S(1)}, bf16[512,256]{1,0:T(8,128)(2,1)S(1)}) custom-call(bf16[512,128]{1,0:T(8,128)(2,1)S(1)} %copy-done.1, bf16[512,128]{1,0:T(8,128)(2,1)S(1)} %copy-done.3, f32[8,16]{1,0:T(8,128)S(1)} %copy-done.6, f32[8,16]{1,0:T(8,128)S(1)} %copy-done.8, f32[1,128]{1,0:T(1,128)S(1)} %bitcast.3), custom_call_target="tpu_custom_call" | custom-call | flops 1000000000 | bytes 4000000 | tf_op jit(solution)/shard_map/near_conv/pallas_call | solution.py:184
  25.0 10.1 %all-to-all-done.got_ref = f32[16,16,128]{2,1,0:T(8,128)S(1)} async-done(((f32[16,16,128]{2,1,0:T(8,128)}), f32[16,16,128]{2,1,0:T(8,128)S(1)}, u32[]{:S(2)}, u32[]{:S(2)}) %all-to-all-start) | async-done | bytes 131104 | tf_op jit(solution)/shard_map/exchange_states/all_to_all | solution.py:182
  35.1 0.0 copy-done.4
  35.1 0.4 gate.1
  35.4 23.9 %all_to_all.10.got_ref = f32[64,4,128]{2,1,0:T(4,128)S(1)} all-to-all(f32[64,4,128]{2,1,0:T(4,128)S(1)} %get-tuple-element.11), channel_id=1, replica_groups=mesh['ctx'=16,'chan'=64] {'chan'}, dimensions={0} | all-to-all | bytes 262144 | tf_op jit(solution)/shard_map/exchange_squares/all_to_all | solution.py:198
  59.4 0.0 copy-start.7
  59.4 0.7 %copy-done.7 = f32[128]{0:T(128)S(1)} copy-done((f32[128]{0:T(128)S(1)}, f32[128]{0:T(128)}, u32[]{:S(2)}) %copy-start.7) | copy-done | bytes 536
  60.0 0.9 %normalize.1 = bf16[512,128]{1,0:T(8,128)(2,1)} custom-call(f32[64,4,128]{2,1,0:T(4,128)S(1)} %all_to_all.10.got_ref, f32[512,128]{1,0:T(8,128)S(1)} %get-tuple-element.12.out_ref, f32[1,128]{1,0:T(1,128)S(1)} %bitcast.2), custom_call_target="tpu_custom_call" | custom-call | flops 1000000 | bytes 1000000 | tf_op jit(solution)/shard_map/normalize/pallas_call | solution.py:200
Async XLA Ops:
  0.0 0.9 %copy-start = (bf16[512,128]{1,0:T(8,128)(2,1)S(1)}, bf16[512,128]{1,0:T(8,128)(2,1)}, u32[]{:S(2)}) copy-start(bf16[512,128]{1,0:T(8,128)(2,1)} %query_ref.3) | copy-start | bytes 393220
  0.9 0.9 %copy-start.2 = (bf16[512,128]{1,0:T(8,128)(2,1)S(1)}, bf16[512,128]{1,0:T(8,128)(2,1)}, u32[]{:S(2)}) copy-start(bf16[512,128]{1,0:T(8,128)(2,1)} %key_ref.3) | copy-start | bytes 393220
  1.8 0.7 %copy-start.5 = (f32[8,16]{1,0:T(8,128)S(1)}, f32[8,16]{1,0:T(8,128)}, u32[]{:S(2)}) copy-start(f32[8,16]{1,0:T(8,128)} %decay_ref.3) | copy-start | bytes 1540
  2.5 20.6 %copy-start.6 = (f32[8,16]{1,0:T(8,128)S(1)}, f32[8,16]{1,0:T(8,128)}, u32[]{:S(2)}) copy-start(f32[8,16]{1,0:T(8,128)} %decay_ref.3) | copy-start | bytes 1540
  2.5 20.6 %copy-start.8 = (f32[8,16]{1,0:T(8,128)S(1)}, f32[8,16]{1,0:T(8,128)}, u32[]{:S(2)}) copy-start(f32[8,16]{1,0:T(8,128)} %residue_ref.1) | copy-start | bytes 1540
  3.5 19.6 %copy-start.1 = (bf16[512,128]{1,0:T(8,128)(2,1)S(1)}, bf16[512,128]{1,0:T(8,128)(2,1)}, u32[]{:S(2)}) copy-start(bf16[512,128]{1,0:T(8,128)(2,1)} %query_ref.3) | copy-start | bytes 393220
  3.5 19.6 %copy-start.3 = (bf16[512,128]{1,0:T(8,128)(2,1)S(1)}, bf16[512,128]{1,0:T(8,128)(2,1)}, u32[]{:S(2)}) copy-start(bf16[512,128]{1,0:T(8,128)(2,1)} %key_ref.3) | copy-start | bytes 393220
  3.5 31.6 %all-to-all-start = ((f32[16,16,128]{2,1,0:T(8,128)}), f32[16,16,128]{2,1,0:T(8,128)S(1)}, u32[]{:S(2)}, u32[]{:S(2)}) async-start(f32[16,16,128]{2,1,0:T(8,128)} %end_state.1), calls=%async_computation | async-start | bytes 262144 | tf_op jit(solution)/shard_map/exchange_states/all_to_all | solution.py:182
  23.1 0.7 %copy-start.9 = (f32[128]{0:T(128)S(1)}, f32[128]{0:T(128)}, u32[]{:S(2)}) copy-start(f32[128]{0:T(128)} %param.12) | copy-start | bytes 1540
  23.7 11.3 %copy-start.4 = (bf16[512,128]{1,0:T(8,128)(2,1)S(1)}, bf16[512,128]{1,0:T(8,128)(2,1)}, u32[]{:S(2)}) copy-start(bf16[512,128]{1,0:T(8,128)(2,1)} %value_ref.1) | copy-start | bytes 393220
  59.4 0.7 %copy-start.7 = (f32[128]{0:T(128)S(1)}, f32[128]{0:T(128)}, u32[]{:S(2)}) copy-start(f32[128]{0:T(128)} %param.13) | copy-start | bytes 1540

commit v2 on v1

--- a/solution.py
+++ b/solution.py
@@ -1,3 +1,5 @@
+import functools
+
 import jax
 import jax.numpy as jnp
 from jax import lax
@@ -8,6 +10,9 @@
 D = 8192
 EPS = 1e-05
 CHUNK = 128
+RUN = 4
+RUN_ORDER = [3, 2, 1, 0]
+CHAN_FIRST = 40
 F32 = jnp.float32
 BF16 = jnp.bfloat16
 VMEM_BYTES = 24 << 20
@@ -62,27 +67,7 @@
     return jnp.sum(full.reshape(groups, rows // groups, width), axis=0)
 
 
-def end_kernel(query_ref, key_ref, decay_ref, send_ref):
-    tokens, width = query_ref.shape
-    groups, modes = decay_ref.shape
-    targets = send_ref.shape[0]
-    me = lax.axis_index("ctx")
-    rate = mode_column(decay_ref[...])
-    mask = own_group(modes, width, width // groups)
-    age = (tokens - 1 - iota((groups * modes, tokens), 1)).astype(F32)
-    lhs = split(jnp.exp(-rate * age))
-    gated = query_ref[...].astype(F32) * key_ref[...].astype(F32)
-    high, low = split(gated)
-    full = dot(lhs[0], high) + (dot(lhs[1], high) + dot(lhs[0], low))
-    state = fold(jnp.where(mask, full, 0.0), groups)
-    block_rate = fold(jnp.where(mask, rate * float(tokens), 0.0), groups)
-    for target in range(targets):
-        between = target - 1 - me
-        decayed = state * jnp.exp(-block_rate * jnp.maximum(between, 0).astype(F32))
-        send_ref[target] = jnp.where(between >= 0, decayed, 0.0)
-
-
-def near_kernel(query_ref, key_ref, decay_ref, residue_ref, skip_ref, near_ref, far_ref):
+def near_part(query_ref, key_ref, decay_ref, residue_ref, skip_ref, near_ref, far_ref):
     tokens, width = query_ref.shape
     groups, modes = decay_ref.shape
     per_group = width // groups
@@ -130,42 +115,105 @@
             state = end if state is None else step * state + end
 
 
-def gate_kernel(got_ref, near_ref, far_ref, value_ref, out_ref, send_ref):
-    tokens, width = near_ref.shape
+def first_run():
+    return lax.axis_index("ctx") < RUN
+
+
+def end_kernel(n, *refs):
+    sources, state_ref, rate_ref = refs[:n], refs[n], refs[n + 1]
+    loaded, (near_ref, far_ref), sems = refs[n + 2 : 2 * n + 2], refs[2 * n + 2 : 2 * n + 4], refs[-1]
+    loads = [pltpu.make_async_copy(a, b, sems.at[i]) for i, (a, b) in enumerate(zip(sources, loaded))]
+    for load in loads:
+        load.start()
+    decay_ref, query_ref, key_ref, residue_ref, skip_ref = loaded[:5]
+    tokens, width = query_ref.shape
+    groups, modes = decay_ref.shape
+    loads[0].wait()
+    rate = mode_column(decay_ref[...])
+    mask = own_group(modes, width, width // groups)
+    age = (tokens - 1 - iota((groups * modes, tokens), 1)).astype(F32)
+    lhs = split(jnp.exp(-rate * age))
+    rate_ref[...] = fold(jnp.where(mask, rate * float(tokens), 0.0), groups)
+    loads[1].wait()
+    loads[2].wait()
+    gated = query_ref[...].astype(F32) * key_ref[...].astype(F32)
+    high, low = split(gated)
+    full = dot(lhs[0], high) + (dot(lhs[1], high) + dot(lhs[0], low))
+    state_ref[...] = fold(jnp.where(mask, full, 0.0), groups)
+    for load in loads[3:]:
+        load.wait()
+
+    @pl.when(first_run())
+    def _():
+        near_part(query_ref, key_ref, decay_ref, residue_ref, skip_ref, near_ref, far_ref)
+
+
+def near_kernel(decay_ref, query_ref, key_ref, residue_ref, skip_ref, after_ref, near_ref, far_ref):
+    @pl.when(jnp.logical_not(first_run()))
+    def _():
+        near_part(query_ref, key_ref, decay_ref, residue_ref, skip_ref, near_ref, far_ref)
+
+
+def step_kernel(own_ref, rate_ref, come_ref, out_ref):
+    out_ref[...] = own_ref[...] + jnp.exp(-rate_ref[...] * float(RUN)) * come_ref[...]
+
+
+def hand_kernel(own_ref, rate_ref, *refs):
+    earlier_refs, send_ref = refs[:-1], refs[-1]
+    place = lax.axis_index("ctx") % RUN
+    block_rate = rate_ref[...]
+    earlier = earlier_refs[0][...]
+    for ref in earlier_refs[1:]:
+        earlier += ref[...]
+    upto = own_ref[...] + jnp.exp(-block_rate * float(RUN)) * earlier
+    for slot in range(RUN):
+        between = RUN_ORDER[slot] - 1 - place
+        own_run = between >= 0
+        age = jnp.where(own_run, between, between + RUN).astype(F32)
+        send_ref[slot] = jnp.where(own_run, upto, earlier) * jnp.exp(-block_rate * age)
+
+
+def gate_kernel(got_ref, near0_ref, far0_ref, near1_ref, far1_ref, value_ref, gain_ref, out_ref, send_ref):
+    tokens, width = value_ref.shape
     modes = got_ref.shape[1]
-    rows = far_ref.shape[1] // 2
-    groups = rows // modes
+    groups = far0_ref.shape[1] // 2 // modes
     state = got_ref[0]
     for source in range(1, got_ref.shape[0]):
         state += got_ref[source]
     mask = own_group(modes, width, width // groups)
-    tiled = jnp.concatenate([state] * groups, axis=0)
-    full = jnp.where(mask, tiled, 0.0)
-    out = value_ref[...].astype(F32) * (near_ref[...] + wide_dot(far_ref[...], full))
-    out_ref[...] = out
-    squares = out * out
-    sums = []
-    for i in range(tokens // CHUNK):
-        turned = jnp.transpose(squares[i * CHUNK : (i + 1) * CHUNK])
-        sums.append(jnp.sum(turned, axis=0, keepdims=True))
-    sums = jnp.concatenate(sums, axis=0)
-    send_ref[...] = jnp.broadcast_to(sums[None], send_ref.shape)
-
-
-def norm_kernel(got_ref, out_ref, gain_ref, mixed_ref):
+    full = jnp.where(mask, jnp.concatenate([state] * groups, axis=0), 0.0)
+
+    def gate(near_ref, far_ref):
+        out = value_ref[...].astype(F32) * (near_ref[...] + wide_dot(far_ref[...], full))
+        out_ref[...] = out * gain_ref[...]
+        squares = out * out
+        sums = []
+        for i in range(tokens // CHUNK):
+            turned = jnp.transpose(squares[i * CHUNK : (i + 1) * CHUNK])
+            sums.append(jnp.sum(turned, axis=0, keepdims=True))
+        sums = jnp.concatenate(sums, axis=0)
+        send_ref[...] = jnp.broadcast_to(sums[None], send_ref.shape)
+
+    first = first_run()
+    pl.when(first)(functools.partial(gate, near0_ref, far0_ref))
+    pl.when(jnp.logical_not(first))(functools.partial(gate, near1_ref, far1_ref))
+
+
+def norm_kernel(got_ref, out_ref, mixed_ref):
     width = out_ref.shape[1]
     total = jnp.sum(got_ref[...], axis=0)
     scale = lax.rsqrt(total / D + EPS)
     for i in range(scale.shape[0]):
         part = pl.ds(i * CHUNK, CHUNK)
         column = jnp.transpose(jnp.broadcast_to(scale[i : i + 1], (width, CHUNK)))
-        mixed_ref[part, :] = (out_ref[part, :] * gain_ref[...] * column).astype(BF16)
-
-
-def call(kernel, outs, flops, size):
+        mixed_ref[part, :] = (out_ref[part, :] * column).astype(BF16)
+
+
+def call(kernel, outs, flops, size, **more):
     return pl.pallas_call(
         kernel,
         out_shape=outs,
+        **more,
         compiler_params=pltpu.CompilerParams(vmem_limit_bytes=VMEM_BYTES),
         cost_estimate=pl.CostEstimate(flops=flops, bytes_accessed=size, transcendentals=0),
     )
@@ -176,30 +224,54 @@
     groups, modes = decay.shape
     ctx, chan = lax.axis_size("ctx"), lax.axis_size("chan")
     shape = jax.ShapeDtypeStruct
+    near_shapes = (shape((tokens, width), F32), shape((tokens, 2 * groups * modes), BF16))
+    inputs = (decay, query, key_in, residue, skip[None, :], value, norm_gain[None, :])
     with jax.named_scope("end_state"):
-        send = call(end_kernel, shape((ctx, modes, width), F32), 10**8, 10**6)(query, key_in, decay)
+        own, block_rate, *loaded, near0, far0 = call(
+            functools.partial(end_kernel, len(inputs)),
+            (
+                *(shape((modes, width), F32),) * 2,
+                *(shape(x.shape, x.dtype) for x in inputs),
+                *near_shapes,
+            ),
+            10**8,
+            10**6,
+            in_specs=[pl.BlockSpec(memory_space=pltpu.HBM)] * len(inputs),
+            scratch_shapes=[pltpu.SemaphoreType.DMA((len(inputs),))],
+        )(*(pltpu.with_memory_space_constraint(x, pltpu.HBM) for x in inputs))
+    *loaded, gate, gain = loaded
+    with jax.named_scope("chain"):
+        upto, earlier = own, []
+        for run in range(1, ctx // RUN):
+            links = [((run - 1) * RUN + i, run * RUN + i) for i in range(RUN)]
+            come = lax.ppermute(upto, "ctx", links)
+            if run == 2:
+                near1, far1 = call(near_kernel, near_shapes, 10**9, 10**6)(*loaded, upto)
+                come, near1, far1 = lax.optimization_barrier((come, near1, far1))
+            earlier.append(come)
+            if run + 1 < ctx // RUN:
+                upto = call(step_kernel, shape((modes, width), F32), 10**5, 10**5)(
+                    own, block_rate, come
+                )
+    with jax.named_scope("hand_over"):
+        send = call(hand_kernel, shape((RUN, modes, width), F32), 10**6, 10**6)(
+            own, block_rate, *earlier
+        )
     with jax.named_scope("exchange_states"):
-        got = lax.all_to_all(send, "ctx", 0, 0)
-    with jax.named_scope("near_conv"):
-        near, far = call(
-            near_kernel,
-            (shape((tokens, width), F32), shape((tokens, 2 * groups * modes), BF16)),
-            10**9,
-            4 * 10**6,
-        )(query, key_in, decay, residue, skip[None, :])
+        runs = [[start + i for i in RUN_ORDER] for start in range(0, ctx, RUN)]
+        got = lax.all_to_all(send, "ctx", 0, 0, axis_index_groups=runs)
     with jax.named_scope("gate"):
         out, send = call(
             gate_kernel,
             (shape((tokens, width), F32), shape((chan, tokens // CHUNK, CHUNK), F32)),
             10**8,
             10**6,
-        )(got, near, far, value)
+        )(got, near0, far0, near1, far1, gate, gain)
     with jax.named_scope("exchange_squares"):
-        got = lax.all_to_all(send, "chan", 0, 0)
+        order = [(i + CHAN_FIRST) % chan for i in range(chan)]
+        got = lax.all_to_all(send, "chan", 0, 0, axis_index_groups=[order])
     with jax.named_scope("normalize"):
-        return call(norm_kernel, shape((tokens, width), BF16), 10**6, 10**6)(
-            got, out, norm_gain[None, :]
-        )
+        return call(norm_kernel, shape((tokens, width), BF16), 10**6, 10**6)(got, out)
 
 
 def solution(mesh):

time: 61.2 us -> 44.5 us (0.73)
  waiting for transfers between devices: 10.1 us -> 0.78 us
  starting transfers between devices: 19.5 us -> 11.5 us
  blocking collectives: 23.9 us -> 28 us
  local copies, waits for them, and re-layouts: 3.78 us -> 0 us
    all_to_all x1 -> x0, starting transfers between devices: 19.5 us -> none  [local(): got = lax.all_to_all(send, 'ctx', 0, 0)]
    ppermute x0 -> x3, starting transfers between devices: none -> 11.5 us  [local(): come = lax.ppermute(upto, 'ctx', links)]
    all_to_all x1 -> x0, waiting for transfers between devices: 10.1 us -> none  [local(): got = lax.all_to_all(send, 'ctx', 0, 0)]
    all_to_all x1 -> x2, blocking collectives: 23.9 us -> 28 us  [the longest x1 18.3 us: local(): got = lax.all_to_all(send, 'chan', 0, 0, axis_index_groups=[order])]
    unnamed x20 -> x0, local copies, waits for them, and re-layouts: 3.78 us -> none
    ppermute x0 -> x3, waiting for transfers between devices: none -> 0.78 us  [local(): come = lax.ppermute(upto, 'ctx', links)]
    pallas_call x3 -> x6, Pallas kernels: 3.11 us -> 3.55 us  [the longest x1 2.61 us: local(): call(functools.partial(end_kernel, len(inputs)), (*(shape((modes, width),...]
  transfers between devices with their start and end apart: 1 -> 3, of which waited for: 1 -> 1; matrix products, arithmetic and copies ran while one was open for 0% -> 0% of each run, Pallas kernels for 2% -> 0%
where the time goes in v2:
time: 44.5 us; the launch traced here: 44.3 us
  blocking collectives  28 us (63%)
  starting transfers between devices  11.5 us (26%)
  Pallas kernels  3.93 us (9%)
  waiting for transfers between devices  0.78 us (2%)
    all_to_all x1, blocking collectives, local(): got = lax.all_to_all(send, 'chan', 0, 0, axis_index_groups=[order])  18.3 us
    ppermute x3, starting transfers between devices, local(): come = lax.ppermute(upto, 'ctx', links)  11.5 us
    all_to_all x1, blocking collectives, local(): got = lax.all_to_all(send, 'ctx', 0, 0, axis_index_groups=runs)  9.68 us
    pallas_call x1, Pallas kernels, local(): call(functools.partial(end_kernel, len(inputs)), (*(shape((modes, width),...  2.61 us
  transfers between devices with their start and end apart: 3, of which 1 were waited for; matrix products, arithmetic and copies ran while one was open for 0% of the time, Pallas kernels for 0%

profile of v2, /device:TPU:1, one launch (start us, length us, event | category | flops | bytes accessed | tf_op | source)
XLA Modules:
  0.0 44.3 jit_solution(15250692105665032223)
XLA Ops:
  0.0 2.6 %end_state.1 = (f32[16,128]{1,0:T(8,128)S(1)}, f32[16,128]{1,0:T(8,128)S(1)}, f32[8,16]{1,0:T(8,128)S(1)}, bf16[512,128]{1,0:T(8,128)(2,1)S(1)}, bf16[512,128]{1...) custom-call(f32[8,16]{1,0:T(8,128)} %refs_0_.1, ...), custom_call_target="tpu_custom_call" | custom-call | flops 100000000 | bytes 1000000 | tf_op jit(solution)/shard_map/end_state/pallas_call | solution.py:230
  2.6 10.2 %collective-permute-start = (f32[16,128]{1,0:T(8,128)S(1)}, f32[16,128]{1,0:T(8,128)S(1)}, u32[]{:S(2)}, u32[]{:S(2)}) collective-permute-start(f32[16,128]{1,0:T(8,128)S(1)} %get-tuple-element.23.own_ref), channel_id=1, source_target_pairs={{0,256},{64,320},{128,384},{192,448},{1,257},{65,321},{129,385},{1... | collective-permute-start | bytes 24584 | tf_op jit(solution)/shard_map/chain/ppermute | solution.py:247
  12.8 0.8 %collective-permute-done.come_ref.refs_0_ = f32[16,128]{1,0:T(8,128)S(1)} collective-permute-done((f32[16,128]{1,0:T(8,128)S(1)}, f32[16,128]{1,0:T(8,128)S(1)}, u32[]{:S(2)}, u32[]{:S(2)}) %collective-permute-start) | collective-permute-done | bytes 8224 | tf_op jit(solution)/shard_map/chain/ppermute | solution.py:247
  13.6 0.7 %collective-permute-start.1 = (f32[16,128]{1,0:T(8,128)S(1)}, f32[16,128]{1,0:T(8,128)S(1)}, u32[]{:S(2)}, u32[]{:S(2)}) collective-permute-start(f32[16,128]{1,0:T(8,128)S(1)} %chain.3.after_ref), channel_id=1, source_target_pairs={{256,512},{320,576},{384,640},{448,704},{257,513},{321,577},{385,6... | collective-permute-start | bytes 24584 | tf_op jit(solution)/shard_map/chain/ppermute | solution.py:247
  14.3 0.0 collective-permute-done.1.come_ref.refs_1_
  14.3 0.7 %collective-permute-start.2 = (f32[16,128]{1,0:T(8,128)S(1)}, f32[16,128]{1,0:T(8,128)S(1)}, u32[]{:S(2)}, u32[]{:S(2)}) collective-permute-start(f32[16,128]{1,0:T(8,128)S(1)} %chain.5), channel_id=1, source_target_pairs={{512,768},{576,832},{640,896},{704,960},{513,769},{577,833},{641,8... | collective-permute-start | bytes 24584 | tf_op jit(solution)/shard_map/chain/ppermute | solution.py:247
  15.0 0.0 collective-permute-done.2.refs_2_
  15.1 9.7 %all_to_all.10.got_ref = f32[4,16,128]{2,1,0:T(8,128)S(1)} all-to-all(f32[4,16,128]{2,1,0:T(8,128)S(1)} %hand_over.1), channel_id=1, replica_groups={{192,128,64,0},{448,384,320,256},{704,640,576,512},{960,896,832,768},{1..., dimensions={0} | all-to-all | bytes 65536 | tf_op jit(solution)/shard_map/exchange_states/all_to_all | solution.py:262
  24.7 0.4 gate.1
  25.1 18.3 %all_to_all.11.got_ref = f32[64,4,128]{2,1,0:T(4,128)S(1)} all-to-all(f32[64,4,128]{2,1,0:T(4,128)S(1)} %get-tuple-element.39), channel_id=1, replica_groups={{40,41,42,43,44,45,46,47,48,49,50,51,52,53,54,55,56,57,58,59,60,61,62,6..., dimensions={0} | all-to-all | bytes 262144 | tf_op jit(solution)/shard_map/exchange_squares/all_to_all | solution.py:272
  43.4 0.9 %normalize.1 = bf16[512,128]{1,0:T(8,128)(2,1)} custom-call(f32[64,4,128]{2,1,0:T(4,128)S(1)} %all_to_all.11.got_ref, f32[512,128]{1,0:T(8,128)S(1)} %get-tuple-element.40.out_ref), custom_call_target="tpu_custom_call" | custom-call | flops 1000000 | bytes 1000000 | tf_op jit(solution)/shard_map/normalize/pallas_call | solution.py:274
  (4 shorter events, 0.1 us)
Async XLA Ops:
  2.6 11.0 %collective-permute-start = (f32[16,128]{1,0:T(8,128)S(1)}, f32[16,128]{1,0:T(8,128)S(1)}, u32[]{:S(2)}, u32[]{:S(2)}) collective-permute-start(f32[16,128]{1,0:T(8,128)S(1)} %get-tuple-element.23.own_ref), channel_id=1, source_target_pairs={{0,256},{64,320},{128,384},{192,448},{1,257},{65,321},{129,385},{1... | collective-permute-start | bytes 24584 | tf_op jit(solution)/shard_map/chain/ppermute | solution.py:247
  13.6 0.7 %collective-permute-start.1 = (f32[16,128]{1,0:T(8,128)S(1)}, f32[16,128]{1,0:T(8,128)S(1)}, u32[]{:S(2)}, u32[]{:S(2)}) collective-permute-start(f32[16,128]{1,0:T(8,128)S(1)} %chain.3.after_ref), channel_id=1, source_target_pairs={{256,512},{320,576},{384,640},{448,704},{257,513},{321,577},{385,6... | collective-permute-start | bytes 24584 | tf_op jit(solution)/shard_map/chain/ppermute | solution.py:247
  14.3 0.7 %collective-permute-start.2 = (f32[16,128]{1,0:T(8,128)S(1)}, f32[16,128]{1,0:T(8,128)S(1)}, u32[]{:S(2)}, u32[]{:S(2)}) collective-permute-start(f32[16,128]{1,0:T(8,128)S(1)} %chain.5), channel_id=1, source_target_pairs={{512,768},{576,832},{640,896},{704,960},{513,769},{577,833},{641,8... | collective-permute-start | bytes 24584 | tf_op jit(solution)/shard_map/chain/ppermute | solution.py:247

commit v3 on v2

--- a/solution.py
+++ b/solution.py
@@ -12,7 +12,7 @@
 CHUNK = 128
 RUN = 4
 RUN_ORDER = [3, 2, 1, 0]
-CHAN_FIRST = 40
+CHAN_FIRST = 41
 F32 = jnp.float32
 BF16 = jnp.bfloat16
 VMEM_BYTES = 24 << 20
@@ -119,33 +119,39 @@
     return lax.axis_index("ctx") < RUN
 
 
-def end_kernel(n, *refs):
-    sources, state_ref, rate_ref = refs[:n], refs[n], refs[n + 1]
-    loaded, (near_ref, far_ref), sems = refs[n + 2 : 2 * n + 2], refs[2 * n + 2 : 2 * n + 4], refs[-1]
-    loads = [pltpu.make_async_copy(a, b, sems.at[i]) for i, (a, b) in enumerate(zip(sources, loaded))]
-    for load in loads:
-        load.start()
-    decay_ref, query_ref, key_ref, residue_ref, skip_ref = loaded[:5]
-    tokens, width = query_ref.shape
-    groups, modes = decay_ref.shape
-    loads[0].wait()
-    rate = mode_column(decay_ref[...])
-    mask = own_group(modes, width, width // groups)
-    age = (tokens - 1 - iota((groups * modes, tokens), 1)).astype(F32)
-    lhs = split(jnp.exp(-rate * age))
-    rate_ref[...] = fold(jnp.where(mask, rate * float(tokens), 0.0), groups)
-    loads[1].wait()
-    loads[2].wait()
-    gated = query_ref[...].astype(F32) * key_ref[...].astype(F32)
-    high, low = split(gated)
-    full = dot(lhs[0], high) + (dot(lhs[1], high) + dot(lhs[0], low))
-    state_ref[...] = fold(jnp.where(mask, full, 0.0), groups)
-    for load in loads[3:]:
-        load.wait()
-
-    @pl.when(first_run())
+def end_kernel(first, n, *refs):
+    sources, state_ref, rate_ref, sems = refs[:n], refs[n], refs[n + 1], refs[-1]
+    loaded = refs[n + 2 : 2 * n + 2]
+    if first:
+        gate_refs, (near_ref, far_ref), loaded = refs[n + 2 : n + 4], refs[n + 4 : n + 6], refs[n + 6 : -1]
+        loaded = (*loaded, *gate_refs)
+
+    @pl.when(first_run() == first)
     def _():
-        near_part(query_ref, key_ref, decay_ref, residue_ref, skip_ref, near_ref, far_ref)
+        loads = [
+            pltpu.make_async_copy(a, b, sems.at[i]) for i, (a, b) in enumerate(zip(sources, loaded))
+        ]
+        for load in loads:
+            load.start()
+        decay_ref, query_ref, key_ref, residue_ref, skip_ref = loaded[:5]
+        tokens, width = query_ref.shape
+        groups, modes = decay_ref.shape
+        loads[0].wait()
+        rate = mode_column(decay_ref[...])
+        mask = own_group(modes, width, width // groups)
+        age = (tokens - 1 - iota((groups * modes, tokens), 1)).astype(F32)
+        lhs = split(jnp.exp(-rate * age))
+        rate_ref[...] = fold(jnp.where(mask, rate * float(tokens), 0.0), groups)
+        loads[1].wait()
+        loads[2].wait()
+        gated = query_ref[...].astype(F32) * key_ref[...].astype(F32)
+        high, low = split(gated)
+        full = dot(lhs[0], high) + (dot(lhs[1], high) + dot(lhs[0], low))
+        state_ref[...] = fold(jnp.where(mask, full, 0.0), groups)
+        for load in loads[3:]:
+            load.wait()
+        if first:
+            near_part(query_ref, key_ref, decay_ref, residue_ref, skip_ref, near_ref, far_ref)
 
 
 def near_kernel(decay_ref, query_ref, key_ref, residue_ref, skip_ref, after_ref, near_ref, far_ref):
@@ -158,32 +164,51 @@
     out_ref[...] = own_ref[...] + jnp.exp(-rate_ref[...] * float(RUN)) * come_ref[...]
 
 
-def hand_kernel(own_ref, rate_ref, *refs):
-    earlier_refs, send_ref = refs[:-1], refs[-1]
+def hand_kernel(own0_ref, rate0_ref, own1_ref, rate1_ref, come_ref, rate_ref, send_ref):
+    first = first_run()
+    block_rate = jnp.where(first, rate0_ref[...], rate1_ref[...])
+    own = jnp.where(first, own0_ref[...], own1_ref[...])
+    come = come_ref[...]
+    rate_ref[...] = block_rate
+    modes = own.shape[0]
+    upto = own + jnp.exp(-block_rate * float(RUN)) * come
+    for slot in range(RUN):
+        send_ref[slot, :modes] = upto
+        send_ref[slot, modes:] = come
+
+
+def run_kernel(got_ref, rate_ref, before_ref, total_ref):
     place = lax.axis_index("ctx") % RUN
     block_rate = rate_ref[...]
-    earlier = earlier_refs[0][...]
-    for ref in earlier_refs[1:]:
-        earlier += ref[...]
-    upto = own_ref[...] + jnp.exp(-block_rate * float(RUN)) * earlier
-    for slot in range(RUN):
-        between = RUN_ORDER[slot] - 1 - place
-        own_run = between >= 0
-        age = jnp.where(own_run, between, between + RUN).astype(F32)
-        send_ref[slot] = jnp.where(own_run, upto, earlier) * jnp.exp(-block_rate * age)
-
-
-def gate_kernel(got_ref, near0_ref, far0_ref, near1_ref, far1_ref, value_ref, gain_ref, out_ref, send_ref):
-    tokens, width = value_ref.shape
-    modes = got_ref.shape[1]
-    groups = far0_ref.shape[1] // 2 // modes
-    state = got_ref[0]
-    for source in range(1, got_ref.shape[0]):
-        state += got_ref[source]
+    modes = block_rate.shape[0]
+    before = jnp.zeros_like(block_rate)
+    total = jnp.zeros_like(block_rate)
+    for slot, source in enumerate(RUN_ORDER):
+        upto, come = got_ref[slot, :modes], got_ref[slot, modes:]
+        between = place - 1 - source
+        inside = between >= 0
+        age = jnp.where(inside, between, between + RUN).astype(F32)
+        before += jnp.where(inside, upto, come) * jnp.exp(-block_rate * age)
+        total += upto * jnp.exp(-block_rate * float(RUN - 1 - source))
+    before_ref[...] = before
+    total_ref[...] = total
+
+
+def gate_kernel(n, before_ref, rate_ref, *refs):
+    come_refs, first_refs, other_refs = refs[:n], refs[n : n + 4], refs[n + 4 : n + 8]
+    out_ref, send_ref = refs[n + 8 :]
+    tokens, width = out_ref.shape
+    modes = rate_ref.shape[0]
+    groups = first_refs[1].shape[1] // 2 // modes
+    come = come_refs[0][...]
+    for ref in come_refs[1:]:
+        come += ref[...]
+    place = (lax.axis_index("ctx") % RUN).astype(F32)
+    state = before_ref[...] + come * jnp.exp(-rate_ref[...] * place)
     mask = own_group(modes, width, width // groups)
     full = jnp.where(mask, jnp.concatenate([state] * groups, axis=0), 0.0)
 
-    def gate(near_ref, far_ref):
+    def gate(near_ref, far_ref, value_ref, gain_ref):
         out = value_ref[...].astype(F32) * (near_ref[...] + wide_dot(far_ref[...], full))
         out_ref[...] = out * gain_ref[...]
         squares = out * out
@@ -195,8 +220,8 @@
         send_ref[...] = jnp.broadcast_to(sums[None], send_ref.shape)
 
     first = first_run()
-    pl.when(first)(functools.partial(gate, near0_ref, far0_ref))
-    pl.when(jnp.logical_not(first))(functools.partial(gate, near1_ref, far1_ref))
+    pl.when(first)(functools.partial(gate, *first_refs))
+    pl.when(jnp.logical_not(first))(functools.partial(gate, *other_refs))
 
 
 def norm_kernel(got_ref, out_ref, mixed_ref):
@@ -226,47 +251,56 @@
     shape = jax.ShapeDtypeStruct
     near_shapes = (shape((tokens, width), F32), shape((tokens, 2 * groups * modes), BF16))
     inputs = (decay, query, key_in, residue, skip[None, :], value, norm_gain[None, :])
-    with jax.named_scope("end_state"):
-        own, block_rate, *loaded, near0, far0 = call(
-            functools.partial(end_kernel, len(inputs)),
+    state_shape = shape((modes, width), F32)
+
+    def end_state(first):
+        kept = len(inputs) - 2 if first else 0
+        return call(
+            functools.partial(end_kernel, first, len(inputs)),
             (
-                *(shape((modes, width), F32),) * 2,
-                *(shape(x.shape, x.dtype) for x in inputs),
-                *near_shapes,
+                state_shape,
+                state_shape,
+                *(shape(x.shape, x.dtype) for x in inputs[kept:]),
+                *(near_shapes if first else ()),
             ),
             10**8,
             10**6,
             in_specs=[pl.BlockSpec(memory_space=pltpu.HBM)] * len(inputs),
-            scratch_shapes=[pltpu.SemaphoreType.DMA((len(inputs),))],
+            scratch_shapes=[
+                *(pltpu.VMEM(x.shape, x.dtype) for x in inputs[:kept]),
+                pltpu.SemaphoreType.DMA((len(inputs),)),
+            ],
         )(*(pltpu.with_memory_space_constraint(x, pltpu.HBM) for x in inputs))
-    *loaded, gate, gain = loaded
+
+    with jax.named_scope("end_state"):
+        own0, rate0, gate0, gain0, near0, far0 = end_state(True)
+        own0, rate0, inputs = lax.optimization_barrier((own0, rate0, inputs))
+        come = lax.ppermute(own0, "ctx", [(i, RUN + i) for i in range(RUN)])
+        own1, rate1, *loaded, gate1, gain1 = end_state(False)
+    with jax.named_scope("exchange_in_run"):
+        block_rate, send = call(
+            hand_kernel, (state_shape, shape((RUN, 2 * modes, width), F32)), 10**5, 10**5
+        )(own0, rate0, own1, rate1, come)
+        runs = [[start + i for i in RUN_ORDER] for start in range(0, ctx, RUN)]
+        got = lax.all_to_all(send, "ctx", 0, 0, axis_index_groups=runs)
+        before, total = call(run_kernel, (state_shape,) * 2, 10**5, 10**5)(got, block_rate)
     with jax.named_scope("chain"):
-        upto, earlier = own, []
-        for run in range(1, ctx // RUN):
+        upto, come = total, []
+        for run in range(2, ctx // RUN):
+            if come:
+                upto = call(step_kernel, state_shape, 10**5, 10**5)(total, block_rate, come[-1])
             links = [((run - 1) * RUN + i, run * RUN + i) for i in range(RUN)]
-            come = lax.ppermute(upto, "ctx", links)
+            come.append(lax.ppermute(upto, "ctx", links))
             if run == 2:
                 near1, far1 = call(near_kernel, near_shapes, 10**9, 10**6)(*loaded, upto)
-                come, near1, far1 = lax.optimization_barrier((come, near1, far1))
-            earlier.append(come)
-            if run + 1 < ctx // RUN:
-                upto = call(step_kernel, shape((modes, width), F32), 10**5, 10**5)(
-                    own, block_rate, come
-                )
-    with jax.named_scope("hand_over"):
-        send = call(hand_kernel, shape((RUN, modes, width), F32), 10**6, 10**6)(
-            own, block_rate, *earlier
-        )
-    with jax.named_scope("exchange_states"):
-        runs = [[start + i for i in RUN_ORDER] for start in range(0, ctx, RUN)]
-        got = lax.all_to_all(send, "ctx", 0, 0, axis_index_groups=runs)
+                come[0], near1, far1 = lax.optimization_barrier((come[0], near1, far1))
     with jax.named_scope("gate"):
         out, send = call(
-            gate_kernel,
+            functools.partial(gate_kernel, len(come)),
             (shape((tokens, width), F32), shape((chan, tokens // CHUNK, CHUNK), F32)),
             10**8,
             10**6,
-        )(got, near0, far0, near1, far1, gate, gain)
+        )(before, block_rate, *come, near0, far0, gate0, gain0, near1, far1, gate1, gain1)
     with jax.named_scope("exchange_squares"):
         order = [(i + CHAN_FIRST) % chan for i in range(chan)]
         got = lax.all_to_all(send, "chan", 0, 0, axis_index_groups=[order])

time: 44.5 us -> 43.6 us (0.980)
  starting transfers between devices: 11.5 us -> 10.2 us
    ppermute x3, starting transfers between devices: 11.5 us -> 10.2 us  [the longest x1 8.92 us: local(): come = lax.ppermute(own0, 'ctx', [(i, RUN + i) for i in range(RUN)])]
    all_to_all x1, blocking collectives: 9.68 us -> 10.1 us  [local(): got = lax.all_to_all(send, 'ctx', 0, 0, axis_index_groups=runs)]
    pallas_call x5 -> x6, Pallas kernels: 3.04 us -> 3.14 us  [the longest x2 2.69 us: end_state(): call(functools.partial(end_kernel, first, len(inputs)), (state_shape, sta...]
where the time goes in v3:
time: 43.6 us; the launch traced here: 43.3 us
  blocking collectives  28.3 us (65%)
  starting transfers between devices  10.2 us (23%)
  Pallas kernels  4.03 us (9%)
  waiting for transfers between devices  0.69 us (2%)
    all_to_all x1, blocking collectives, local(): got = lax.all_to_all(send, 'chan', 0, 0, axis_index_groups=[order])  18.2 us
    all_to_all x1, blocking collectives, local(): got = lax.all_to_all(send, 'ctx', 0, 0, axis_index_groups=runs)  10.1 us
    ppermute x1, starting transfers between devices, local(): come = lax.ppermute(own0, 'ctx', [(i, RUN + i) for i in range(RUN)])  8.92 us
    pallas_call x2, Pallas kernels, end_state(): call(functools.partial(end_kernel, first, len(inputs)), (state_shape, sta...  2.69 us
    ppermute x2, starting transfers between devices, local(): come.append(lax.ppermute(upto, 'ctx', links))  1.32 us
  transfers between devices with their start and end apart: 3, of which 1 were waited for; matrix products, arithmetic and copies ran while one was open for 0% of the time, Pallas kernels for 0%

profile of v3, /device:TPU:1, one launch (start us, length us, event | category | flops | bytes accessed | tf_op | source)
XLA Modules:
  0.0 43.3 jit_solution(13309536468016630047)
XLA Ops:
  0.0 2.6 %end_state.2 = (f32[16,128]{1,0:T(8,128)S(1)}, f32[16,128]{1,0:T(8,128)S(1)}, bf16[512,128]{1,0:T(8,128)(2,1)S(1)}, f32[1,128]{1,0:T(1,128)S(1)}, f32[512,128]{1,0:T(8,128)S(1)}, /*index=5*/bf16[512,256]{1,0:T(8,128)(2,1)S(1)}) custom-call(f32[8,16]{1,0:T(8,128)} %refs_0_.2, bf16[512,128]{1,0:T(8,128)(2,1)} %refs_1_.2, bf16[512,128]{1,0:T(8,128)(2,1)} %refs_2_.2, ...), custom_call_target="tpu_custom_call" | custom-call | flops 100000000 | bytes 1000000 | tf_op jit(solution)/shard_map/end_state/pallas_call | solution.py:258
  2.6 8.9 %collective-permute-start = (f32[16,128]{1,0:T(8,128)S(1)}, f32[16,128]{1,0:T(8,128)S(1)}, u32[]{:S(2)}, u32[]{:S(2)}) collective-permute-start(f32[16,128]{1,0:T(8,128)S(1)} %get-tuple-element.42.own0_ref), channel_id=1, source_target_pairs={{0,256},{64,320},{128,384},{192,448},{1,257},{65,321},{129,385},{1... | collective-permute-start | bytes 24584 | tf_op jit(solution)/shard_map/end_state/ppermute | solution.py:278
  11.5 0.1 end_state.3
  11.6 0.7 %collective-permute-done.come_ref = f32[16,128]{1,0:T(8,128)S(1)} collective-permute-done((f32[16,128]{1,0:T(8,128)S(1)}, f32[16,128]{1,0:T(8,128)S(1)}, u32[]{:S(2)}, u32[]{:S(2)}) %collective-permute-start) | collective-permute-done | bytes 8224 | tf_op jit(solution)/shard_map/end_state/ppermute | solution.py:278
  12.3 10.1 %all_to_all.10.got_ref = f32[4,32,128]{2,1,0:T(8,128)S(1)} all-to-all(f32[4,32,128]{2,1,0:T(8,128)S(1)} %get-tuple-element.53), channel_id=1, replica_groups={{192,128,64,0},{448,384,320,256},{704,640,576,512},{960,896,832,768},{1..., dimensions={0} | all-to-all | bytes 131072 | tf_op jit(solution)/shard_map/exchange_in_run/all_to_all | solution.py:285
  22.5 0.7 %collective-permute-start.1 = (f32[16,128]{1,0:T(8,128)S(1)}, f32[16,128]{1,0:T(8,128)S(1)}, u32[]{:S(2)}, u32[]{:S(2)}) collective-permute-start(f32[16,128]{1,0:T(8,128)S(1)} %get-tuple-element.56.after_ref.own_ref), channel_id=1, source_target_pairs={{256,512},{320,576},{384,640},{448,704},{257,513},{321,577},{385,6... | collective-permute-start | bytes 24584 | tf_op jit(solution)/shard_map/chain/ppermute | solution.py:293
  23.2 0.0 collective-permute-done.1.come_ref.refs_0_
  23.2 0.7 %collective-permute-start.2 = (f32[16,128]{1,0:T(8,128)S(1)}, f32[16,128]{1,0:T(8,128)S(1)}, u32[]{:S(2)}, u32[]{:S(2)}) collective-permute-start(f32[16,128]{1,0:T(8,128)S(1)} %chain.3), channel_id=1, source_target_pairs={{512,768},{576,832},{640,896},{704,960},{513,769},{577,833},{641,8... | collective-permute-start | bytes 24584 | tf_op jit(solution)/shard_map/chain/ppermute | solution.py:293
  23.9 0.0 collective-permute-done.2.refs_1_
  23.9 0.4 gate.1
  24.3 18.2 %all_to_all.11.got_ref = f32[64,4,128]{2,1,0:T(4,128)S(1)} all-to-all(f32[64,4,128]{2,1,0:T(4,128)S(1)} %get-tuple-element.73), channel_id=1, replica_groups={{41,42,43,44,45,46,47,48,49,50,51,52,53,54,55,56,57,58,59,60,61,62,63,0..., dimensions={0} | all-to-all | bytes 262144 | tf_op jit(solution)/shard_map/exchange_squares/all_to_all | solution.py:306
  42.5 0.9 %normalize.1 = bf16[512,128]{1,0:T(8,128)(2,1)} custom-call(f32[64,4,128]{2,1,0:T(4,128)S(1)} %all_to_all.11.got_ref, f32[512,128]{1,0:T(8,128)S(1)} %get-tuple-element.74.out_ref), custom_call_target="tpu_custom_call" | custom-call | flops 1000000 | bytes 1000000 | tf_op jit(solution)/shard_map/normalize/pallas_call | solution.py:308
  (4 shorter events, 0.1 us)
Async XLA Ops:
  2.6 9.7 %collective-permute-start = (f32[16,128]{1,0:T(8,128)S(1)}, f32[16,128]{1,0:T(8,128)S(1)}, u32[]{:S(2)}, u32[]{:S(2)}) collective-permute-start(f32[16,128]{1,0:T(8,128)S(1)} %get-tuple-element.42.own0_ref), channel_id=1, source_target_pairs={{0,256},{64,320},{128,384},{192,448},{1,257},{65,321},{129,385},{1... | collective-permute-start | bytes 24584 | tf_op jit(solution)/shard_map/end_state/ppermute | solution.py:278
  22.5 0.7 %collective-permute-start.1 = (f32[16,128]{1,0:T(8,128)S(1)}, f32[16,128]{1,0:T(8,128)S(1)}, u32[]{:S(2)}, u32[]{:S(2)}) collective-permute-start(f32[16,128]{1,0:T(8,128)S(1)} %get-tuple-element.56.after_ref.own_ref), channel_id=1, source_target_pairs={{256,512},{320,576},{384,640},{448,704},{257,513},{321,577},{385,6... | collective-permute-start | bytes 24584 | tf_op jit(solution)/shard_map/chain/ppermute | solution.py:293
  23.2 0.7 %collective-permute-start.2 = (f32[16,128]{1,0:T(8,128)S(1)}, f32[16,128]{1,0:T(8,128)S(1)}, u32[]{:S(2)}, u32[]{:S(2)}) collective-permute-start(f32[16,128]{1,0:T(8,128)S(1)} %chain.3), channel_id=1, source_target_pairs={{512,768},{576,832},{640,896},{704,960},{513,769},{577,833},{641,8... | collective-permute-start | bytes 24584 | tf_op jit(solution)/shard_map/chain/ppermute | solution.py:293

commit v4 on v3

--- a/solution.py
+++ b/solution.py
@@ -67,7 +67,7 @@
     return jnp.sum(full.reshape(groups, rows // groups, width), axis=0)
 
 
-def near_part(query_ref, key_ref, decay_ref, residue_ref, skip_ref, near_ref, far_ref):
+def near_part(decay_ref, query_ref, key_ref, residue_ref, skip_ref, near_ref, far_ref):
     tokens, width = query_ref.shape
     groups, modes = decay_ref.shape
     per_group = width // groups
@@ -119,45 +119,47 @@
     return lax.axis_index("ctx") < RUN
 
 
-def end_kernel(first, n, *refs):
-    sources, state_ref, rate_ref, sems = refs[:n], refs[n], refs[n + 1], refs[-1]
-    loaded = refs[n + 2 : 2 * n + 2]
-    if first:
-        gate_refs, (near_ref, far_ref), loaded = refs[n + 2 : n + 4], refs[n + 4 : n + 6], refs[n + 6 : -1]
-        loaded = (*loaded, *gate_refs)
-
-    @pl.when(first_run() == first)
+def end_state(sources, state_ref, rate_ref, loaded, sems):
+    loads = [pltpu.make_async_copy(a, b, sems.at[i]) for i, (a, b) in enumerate(zip(sources, loaded))]
+    for load in loads:
+        load.start()
+    decay_ref, query_ref, key_ref = loaded[:3]
+    tokens, width = query_ref.shape
+    groups, modes = decay_ref.shape
+    loads[0].wait()
+    rate = mode_column(decay_ref[...])
+    mask = own_group(modes, width, width // groups)
+    age = (tokens - 1 - iota((groups * modes, tokens), 1)).astype(F32)
+    lhs = split(jnp.exp(-rate * age))
+    rate_ref[...] = fold(jnp.where(mask, rate * float(tokens), 0.0), groups)
+    loads[1].wait()
+    loads[2].wait()
+    gated = query_ref[...].astype(F32) * key_ref[...].astype(F32)
+    high, low = split(gated)
+    full = dot(lhs[0], high) + (dot(lhs[1], high) + dot(lhs[0], low))
+    state_ref[...] = fold(jnp.where(mask, full, 0.0), groups)
+    for load in loads[3:]:
+        load.wait()
+
+
+def first_kernel(n, *refs):
+    @pl.when(first_run())
     def _():
-        loads = [
-            pltpu.make_async_copy(a, b, sems.at[i]) for i, (a, b) in enumerate(zip(sources, loaded))
-        ]
-        for load in loads:
-            load.start()
-        decay_ref, query_ref, key_ref, residue_ref, skip_ref = loaded[:5]
-        tokens, width = query_ref.shape
-        groups, modes = decay_ref.shape
-        loads[0].wait()
-        rate = mode_column(decay_ref[...])
-        mask = own_group(modes, width, width // groups)
-        age = (tokens - 1 - iota((groups * modes, tokens), 1)).astype(F32)
-        lhs = split(jnp.exp(-rate * age))
-        rate_ref[...] = fold(jnp.where(mask, rate * float(tokens), 0.0), groups)
-        loads[1].wait()
-        loads[2].wait()
-        gated = query_ref[...].astype(F32) * key_ref[...].astype(F32)
-        high, low = split(gated)
-        full = dot(lhs[0], high) + (dot(lhs[1], high) + dot(lhs[0], low))
-        state_ref[...] = fold(jnp.where(mask, full, 0.0), groups)
-        for load in loads[3:]:
-            load.wait()
-        if first:
-            near_part(query_ref, key_ref, decay_ref, residue_ref, skip_ref, near_ref, far_ref)
+        end_state(refs[:n], refs[n], refs[n + 1], refs[n + 2 : -1], refs[-1])
+
+
+def other_kernel(n, *refs):
+    sources, ready, refs, sems = refs[:n], refs[n : n + 5], refs[n + 5 : -1], refs[-1]
+    first = first_run()
+    pl.when(first)(functools.partial(near_part, *ready, *refs[-2:]))
+    others = functools.partial(end_state, sources, refs[0], refs[1], refs[2:-2], sems)
+    pl.when(jnp.logical_not(first))(others)
 
 
 def near_kernel(decay_ref, query_ref, key_ref, residue_ref, skip_ref, after_ref, near_ref, far_ref):
     @pl.when(jnp.logical_not(first_run()))
     def _():
-        near_part(query_ref, key_ref, decay_ref, residue_ref, skip_ref, near_ref, far_ref)
+        near_part(decay_ref, query_ref, key_ref, residue_ref, skip_ref, near_ref, far_ref)
 
 
 def step_kernel(own_ref, rate_ref, come_ref, out_ref):
@@ -253,30 +255,26 @@
     inputs = (decay, query, key_in, residue, skip[None, :], value, norm_gain[None, :])
     state_shape = shape((modes, width), F32)
 
-    def end_state(first):
-        kept = len(inputs) - 2 if first else 0
+    in_hbm = [pltpu.with_memory_space_constraint(x, pltpu.HBM) for x in inputs]
+
+    def ends(kernel, ready, more):
+        n = len(inputs)
         return call(
-            functools.partial(end_kernel, first, len(inputs)),
-            (
-                state_shape,
-                state_shape,
-                *(shape(x.shape, x.dtype) for x in inputs[kept:]),
-                *(near_shapes if first else ()),
-            ),
+            functools.partial(kernel, n),
+            (state_shape, state_shape, *(shape(x.shape, x.dtype) for x in inputs), *more),
             10**8,
             10**6,
-            in_specs=[pl.BlockSpec(memory_space=pltpu.HBM)] * len(inputs),
-            scratch_shapes=[
-                *(pltpu.VMEM(x.shape, x.dtype) for x in inputs[:kept]),
-                pltpu.SemaphoreType.DMA((len(inputs),)),
+            in_specs=[
+                *[pl.BlockSpec(memory_space=pltpu.HBM)] * n,
+                *[pl.BlockSpec(memory_space=pltpu.VMEM)] * len(ready),
             ],
-        )(*(pltpu.with_memory_space_constraint(x, pltpu.HBM) for x in inputs))
+            scratch_shapes=[pltpu.SemaphoreType.DMA((n,))],
+        )(*in_hbm, *ready)
 
     with jax.named_scope("end_state"):
-        own0, rate0, gate0, gain0, near0, far0 = end_state(True)
-        own0, rate0, inputs = lax.optimization_barrier((own0, rate0, inputs))
+        own0, rate0, *loaded0, gate0, gain0 = ends(first_kernel, (), ())
         come = lax.ppermute(own0, "ctx", [(i, RUN + i) for i in range(RUN)])
-        own1, rate1, *loaded, gate1, gain1 = end_state(False)
+        own1, rate1, *loaded, gate1, gain1, near0, far0 = ends(other_kernel, loaded0, near_shapes)
     with jax.named_scope("exchange_in_run"):
         block_rate, send = call(
             hand_kernel, (state_shape, shape((RUN, 2 * modes, width), F32)), 10**5, 10**5

time: 43.6 us -> 43 us (0.986)
  starting transfers between devices: 10.2 us -> 11.5 us
  blocking collectives: 28.3 us -> 27.1 us
  waiting for transfers between devices: 0.69 us -> 0.01 us
    ppermute x1, starting transfers between devices: 8.92 us -> 10.2 us  [local(): come = lax.ppermute(own0, 'ctx', [(i, RUN + i) for i in range(RUN)])]
    all_to_all x1, blocking collectives: 18.2 us -> 17 us  [local(): got = lax.all_to_all(send, 'chan', 0, 0, axis_index_groups=[order])]
    ppermute x1, waiting for transfers between devices: 0.68 us -> 0.01 us  [local(): come = lax.ppermute(own0, 'ctx', [(i, RUN + i) for i in range(RUN)])]
  transfers between devices with their start and end apart: 3 -> 3, of which waited for: 1 -> 0; matrix products, arithmetic and copies ran while one was open for 0% -> 0% of each run, Pallas kernels for 0% -> 3%
where the time goes in v4:
time: 43 us; the launch traced here: 42.7 us
  blocking collectives  27.1 us (63%)
  starting transfers between devices  11.5 us (27%)
  Pallas kernels  4.04 us (9%)
    all_to_all x1, blocking collectives, local(): got = lax.all_to_all(send, 'chan', 0, 0, axis_index_groups=[order])  17 us
    ppermute x1, starting transfers between devices, local(): come = lax.ppermute(own0, 'ctx', [(i, RUN + i) for i in range(RUN)])  10.2 us
    all_to_all x1, blocking collectives, local(): got = lax.all_to_all(send, 'ctx', 0, 0, axis_index_groups=runs)  10.1 us
    pallas_call x2, Pallas kernels, ends(): call(functools.partial(kernel, n), (state_shape, state_shape, *(shape(x.s...  2.69 us
    ppermute x2, starting transfers between devices, local(): come.append(lax.ppermute(upto, 'ctx', links))  1.32 us
    pallas_call x1, Pallas kernels, local(): call(norm_kernel, shape((tokens, width), BF16), 10 ** 6, 10 ** 6)(got, out)  0.87 us
  transfers between devices with their start and end apart: 3, of which 0 were waited for; matrix products, arithmetic and copies ran while one was open for 0% of the time, Pallas kernels for 3%

profile of v4, /device:TPU:1, one launch (start us, length us, event | category | flops | bytes accessed | tf_op | source)
XLA Modules:
  0.0 42.7 jit_solution(268773493204997108)
XLA Ops:
  0.0 1.3 %end_state.2 = (f32[16,128]{1,0:T(8,128)S(1)}, f32[16,128]{1,0:T(8,128)S(1)}, f32[8,16]{1,0:T(8,128)S(1)}, bf16[512,128]{1,0:T(8,128)(2,1)S(1)}, bf16[512,128]{1...) custom-call(f32[8,16]{1,0:T(8,128)} %refs_0_.3, ...), custom_call_target="tpu_custom_call" | custom-call | flops 100000000 | bytes 1000000 | tf_op jit(solution)/shard_map/end_state/pallas_call | solution.py:262
  1.4 10.2 %collective-permute-start = (f32[16,128]{1,0:T(8,128)S(1)}, f32[16,128]{1,0:T(8,128)S(1)}, u32[]{:S(2)}, u32[]{:S(2)}) collective-permute-start(f32[16,128]{1,0:T(8,128)S(1)} %get-tuple-element.36.own0_ref), channel_id=1, source_target_pairs={{0,256},{64,320},{128,384},{192,448},{1,257},{65,321},{129,385},{1... | collective-permute-start | bytes 24584 | tf_op jit(solution)/shard_map/end_state/ppermute | solution.py:276
  11.5 1.3 %end_state.3 = (f32[16,128]{1,0:T(8,128)S(1)}, f32[16,128]{1,0:T(8,128)S(1)}, f32[8,16]{1,0:T(8,128)S(1)}, bf16[512,128]{1,0:T(8,128)(2,1)S(1)}, bf16[512,128]{1...) custom-call(f32[8,16]{1,0:T(8,128)} %refs_0_.3, ...), custom_call_target="tpu_custom_call" | custom-call | flops 100000000 | bytes 1000000 | tf_op jit(solution)/shard_map/end_state/pallas_call | solution.py:262
  12.9 0.0 collective-permute-done.come_ref
  12.9 10.1 %all_to_all.10.got_ref = f32[4,32,128]{2,1,0:T(8,128)S(1)} all-to-all(f32[4,32,128]{2,1,0:T(8,128)S(1)} %get-tuple-element.45), channel_id=1, replica_groups={{192,128,64,0},{448,384,320,256},{704,640,576,512},{960,896,832,768},{1..., dimensions={0} | all-to-all | bytes 131072 | tf_op jit(solution)/shard_map/exchange_in_run/all_to_all | solution.py:283
  23.1 0.7 %collective-permute-start.1 = (f32[16,128]{1,0:T(8,128)S(1)}, f32[16,128]{1,0:T(8,128)S(1)}, u32[]{:S(2)}, u32[]{:S(2)}) collective-permute-start(f32[16,128]{1,0:T(8,128)S(1)} %get-tuple-element.48.after_ref.own_ref), channel_id=1, source_target_pairs={{256,512},{320,576},{384,640},{448,704},{257,513},{321,577},{385,6... | collective-permute-start | bytes 24584 | tf_op jit(solution)/shard_map/chain/ppermute | solution.py:291
  23.8 0.0 collective-permute-done.1.come_ref.refs_0_
  23.8 0.7 %collective-permute-start.2 = (f32[16,128]{1,0:T(8,128)S(1)}, f32[16,128]{1,0:T(8,128)S(1)}, u32[]{:S(2)}, u32[]{:S(2)}) collective-permute-start(f32[16,128]{1,0:T(8,128)S(1)} %chain.3), channel_id=1, source_target_pairs={{512,768},{576,832},{640,896},{704,960},{513,769},{577,833},{641,8... | collective-permute-start | bytes 24584 | tf_op jit(solution)/shard_map/chain/ppermute | solution.py:291
  24.5 0.0 collective-permute-done.2.refs_1_
  24.5 0.4 gate.1
  24.9 17.0 %all_to_all.11.got_ref = f32[64,4,128]{2,1,0:T(4,128)S(1)} all-to-all(f32[64,4,128]{2,1,0:T(4,128)S(1)} %get-tuple-element.65), channel_id=1, replica_groups={{41,42,43,44,45,46,47,48,49,50,51,52,53,54,55,56,57,58,59,60,61,62,63,0..., dimensions={0} | all-to-all | bytes 262144 | tf_op jit(solution)/shard_map/exchange_squares/all_to_all | solution.py:304
  41.9 0.9 %normalize.1 = bf16[512,128]{1,0:T(8,128)(2,1)} custom-call(f32[64,4,128]{2,1,0:T(4,128)S(1)} %all_to_all.11.got_ref, f32[512,128]{1,0:T(8,128)S(1)} %get-tuple-element.66.out_ref), custom_call_target="tpu_custom_call" | custom-call | flops 1000000 | bytes 1000000 | tf_op jit(solution)/shard_map/normalize/pallas_call | solution.py:306
  (4 shorter events, 0.1 us)
Async XLA Ops:
  1.4 11.5 %collective-permute-start = (f32[16,128]{1,0:T(8,128)S(1)}, f32[16,128]{1,0:T(8,128)S(1)}, u32[]{:S(2)}, u32[]{:S(2)}) collective-permute-start(f32[16,128]{1,0:T(8,128)S(1)} %get-tuple-element.36.own0_ref), channel_id=1, source_target_pairs={{0,256},{64,320},{128,384},{192,448},{1,257},{65,321},{129,385},{1... | collective-permute-start | bytes 24584 | tf_op jit(solution)/shard_map/end_state/ppermute | solution.py:276
  23.1 0.7 %collective-permute-start.1 = (f32[16,128]{1,0:T(8,128)S(1)}, f32[16,128]{1,0:T(8,128)S(1)}, u32[]{:S(2)}, u32[]{:S(2)}) collective-permute-start(f32[16,128]{1,0:T(8,128)S(1)} %get-tuple-element.48.after_ref.own_ref), channel_id=1, source_target_pairs={{256,512},{320,576},{384,640},{448,704},{257,513},{321,577},{385,6... | collective-permute-start | bytes 24584 | tf_op jit(solution)/shard_map/chain/ppermute | solution.py:291
  23.8 0.7 %collective-permute-start.2 = (f32[16,128]{1,0:T(8,128)S(1)}, f32[16,128]{1,0:T(8,128)S(1)}, u32[]{:S(2)}, u32[]{:S(2)}) collective-permute-start(f32[16,128]{1,0:T(8,128)S(1)} %chain.3), channel_id=1, source_target_pairs={{512,768},{576,832},{640,896},{704,960},{513,769},{577,833},{641,8... | collective-permute-start | bytes 24584 | tf_op jit(solution)/shard_map/chain/ppermute | solution.py:291

commit v5 on v4

--- a/solution.py
+++ b/solution.py
@@ -166,14 +166,16 @@
     out_ref[...] = own_ref[...] + jnp.exp(-rate_ref[...] * float(RUN)) * come_ref[...]
 
 
-def hand_kernel(own0_ref, rate0_ref, own1_ref, rate1_ref, come_ref, rate_ref, send_ref):
+def hand_kernel(
+    own0_ref, rate0_ref, own1_ref, rate1_ref, come_ref, oldest_ref, rate_ref, send_ref
+):
     first = first_run()
     block_rate = jnp.where(first, rate0_ref[...], rate1_ref[...])
     own = jnp.where(first, own0_ref[...], own1_ref[...])
-    come = come_ref[...]
+    come = come_ref[...] + jnp.exp(-block_rate) * oldest_ref[...]
     rate_ref[...] = block_rate
     modes = own.shape[0]
-    upto = own + jnp.exp(-block_rate * float(RUN)) * come
+    upto = own + jnp.exp(-block_rate * float(RUN - 1)) * come
     for slot in range(RUN):
         send_ref[slot, :modes] = upto
         send_ref[slot, modes:] = come
@@ -189,7 +191,7 @@
         upto, come = got_ref[slot, :modes], got_ref[slot, modes:]
         between = place - 1 - source
         inside = between >= 0
-        age = jnp.where(inside, between, between + RUN).astype(F32)
+        age = jnp.maximum(jnp.where(inside, between, between + RUN - 1), 0).astype(F32)
         before += jnp.where(inside, upto, come) * jnp.exp(-block_rate * age)
         total += upto * jnp.exp(-block_rate * float(RUN - 1 - source))
     before_ref[...] = before
@@ -227,13 +229,15 @@
 
 
 def norm_kernel(got_ref, out_ref, mixed_ref):
-    width = out_ref.shape[1]
-    total = jnp.sum(got_ref[...], axis=0)
-    scale = lax.rsqrt(total / D + EPS)
+    parts = got_ref[...]
+    while parts.shape[0] > 1:
+        half = parts.shape[0] // 2
+        parts = parts[:half] + parts[half:]
+    scale = lax.rsqrt(parts[0] / D + EPS)
+    columns = jnp.transpose(jnp.concatenate([scale, scale], axis=0))
     for i in range(scale.shape[0]):
         part = pl.ds(i * CHUNK, CHUNK)
-        column = jnp.transpose(jnp.broadcast_to(scale[i : i + 1], (width, CHUNK)))
-        mixed_ref[part, :] = (out_ref[part, :] * column).astype(BF16)
+        mixed_ref[part, :] = (out_ref[part, :] * columns[:, i : i + 1]).astype(BF16)
 
 
 def call(kernel, outs, flops, size, **more):
@@ -273,12 +277,13 @@
 
     with jax.named_scope("end_state"):
         own0, rate0, *loaded0, gate0, gain0 = ends(first_kernel, (), ())
-        come = lax.ppermute(own0, "ctx", [(i, RUN + i) for i in range(RUN)])
+        oldest = lax.ppermute(own0, "ctx", [(0, RUN)])
+        come = lax.ppermute(own0, "ctx", [(i, RUN - 1 + i) for i in range(1, RUN)])
         own1, rate1, *loaded, gate1, gain1, near0, far0 = ends(other_kernel, loaded0, near_shapes)
     with jax.named_scope("exchange_in_run"):
         block_rate, send = call(
             hand_kernel, (state_shape, shape((RUN, 2 * modes, width), F32)), 10**5, 10**5
-        )(own0, rate0, own1, rate1, come)
+        )(own0, rate0, own1, rate1, come, oldest)
         runs = [[start + i for i in RUN_ORDER] for start in range(0, ctx, RUN)]
         got = lax.all_to_all(send, "ctx", 0, 0, axis_index_groups=runs)
         before, total = call(run_kernel, (state_shape,) * 2, 10**5, 10**5)(got, block_rate)

time: 43 us -> 43.1 us (level)
  starting transfers between devices: 11.5 us -> 12.2 us
  blocking collectives: 27.1 us -> 26.5 us
    all_to_all x1, blocking collectives: 10.1 us -> 8.32 us  [local(): got = lax.all_to_all(send, 'ctx', 0, 0, axis_index_groups=runs)]
    all_to_all x1, blocking collectives: 17 us -> 18.1 us  [local(): got = lax.all_to_all(send, 'chan', 0, 0, axis_index_groups=[order])]
    ppermute x1 -> x2, starting transfers between devices: 10.2 us -> 10.8 us  [the longest x1 10.2 us: local(): oldest = lax.ppermute(own0, 'ctx', [(0, RUN)])]
  transfers between devices with their start and end apart: 3 -> 4, of which waited for: 0 -> 0; matrix products, arithmetic and copies ran while one was open for 0% -> 0% of each run, Pallas kernels for 3% -> 3%
where the time goes in v5:
time: 43.1 us; the launch traced here: 42.9 us
  blocking collectives  26.5 us (61%)
  starting transfers between devices  12.2 us (28%)
  Pallas kernels  4.1 us (10%)
    all_to_all x1, blocking collectives, local(): got = lax.all_to_all(send, 'chan', 0, 0, axis_index_groups=[order])  18.1 us
    ppermute x1, starting transfers between devices, local(): oldest = lax.ppermute(own0, 'ctx', [(0, RUN)])  10.2 us
    all_to_all x1, blocking collectives, local(): got = lax.all_to_all(send, 'ctx', 0, 0, axis_index_groups=runs)  8.32 us
    pallas_call x2, Pallas kernels, ends(): call(functools.partial(kernel, n), (state_shape, state_shape, *(shape(x.s...  2.69 us
    ppermute x2, starting transfers between devices, local(): come.append(lax.ppermute(upto, 'ctx', links))  1.32 us
    pallas_call x1, Pallas kernels, local(): call(norm_kernel, shape((tokens, width), BF16), 10 ** 6, 10 ** 6)(got, out)  0.94 us
  transfers between devices with their start and end apart: 4, of which 0 were waited for; matrix products, arithmetic and copies ran while one was open for 0% of the time, Pallas kernels for 3%

profile of v5, /device:TPU:1, one launch (start us, length us, event | category | flops | bytes accessed | tf_op | source)
XLA Modules:
  0.0 42.9 jit_solution(6878600930865118128)
XLA Ops:
  0.0 1.3 %end_state.2 = (f32[16,128]{1,0:T(8,128)S(1)}, f32[16,128]{1,0:T(8,128)S(1)}, f32[8,16]{1,0:T(8,128)S(1)}, bf16[512,128]{1,0:T(8,128)(2,1)S(1)}, bf16[512,128]{1...) custom-call(f32[8,16]{1,0:T(8,128)} %refs_0_.3, ...), custom_call_target="tpu_custom_call" | custom-call | flops 100000000 | bytes 1000000 | tf_op jit(solution)/shard_map/end_state/pallas_call | solution.py:266
  1.4 10.2 %collective-permute-start.1 = (f32[16,128]{1,0:T(8,128)S(1)}, f32[16,128]{1,0:T(8,128)S(1)}, u32[]{:S(2)}, u32[]{:S(2)}) collective-permute-start(f32[16,128]{1,0:T(8,128)S(1)} %get-tuple-element.36.own0_ref), channel_id=1, source_target_pairs={{0,256},{1,257},{2,258},{3,259},{4,260},{5,261},{6,262},{7,263},{8... | collective-permute-start | bytes 24584 | tf_op jit(solution)/shard_map/end_state/ppermute | solution.py:280
  11.5 0.7 %collective-permute-start = (f32[16,128]{1,0:T(8,128)S(1)}, f32[16,128]{1,0:T(8,128)S(1)}, u32[]{:S(2)}, u32[]{:S(2)}) collective-permute-start(f32[16,128]{1,0:T(8,128)S(1)} %get-tuple-element.36.own0_ref), channel_id=1, source_target_pairs={{64,256},{128,320},{192,384},{65,257},{129,321},{193,385},{66,258}... | collective-permute-start | bytes 24584 | tf_op jit(solution)/shard_map/end_state/ppermute | solution.py:281
  12.2 1.3 %end_state.3 = (f32[16,128]{1,0:T(8,128)S(1)}, f32[16,128]{1,0:T(8,128)S(1)}, f32[8,16]{1,0:T(8,128)S(1)}, bf16[512,128]{1,0:T(8,128)(2,1)S(1)}, bf16[512,128]{1...) custom-call(f32[8,16]{1,0:T(8,128)} %refs_0_.3, ...), custom_call_target="tpu_custom_call" | custom-call | flops 100000000 | bytes 1000000 | tf_op jit(solution)/shard_map/end_state/pallas_call | solution.py:266
  13.6 0.0 collective-permute-done.1.oldest_ref
  13.6 0.0 collective-permute-done.come_ref
  13.6 8.3 %all_to_all.10.got_ref = f32[4,32,128]{2,1,0:T(8,128)S(1)} all-to-all(f32[4,32,128]{2,1,0:T(8,128)S(1)} %get-tuple-element.45), channel_id=1, replica_groups={{192,128,64,0},{448,384,320,256},{704,640,576,512},{960,896,832,768},{1..., dimensions={0} | all-to-all | bytes 131072 | tf_op jit(solution)/shard_map/exchange_in_run/all_to_all | solution.py:288
  22.0 0.7 %collective-permute-start.2 = (f32[16,128]{1,0:T(8,128)S(1)}, f32[16,128]{1,0:T(8,128)S(1)}, u32[]{:S(2)}, u32[]{:S(2)}) collective-permute-start(f32[16,128]{1,0:T(8,128)S(1)} %get-tuple-element.48.after_ref.own_ref), channel_id=1, source_target_pairs={{256,512},{320,576},{384,640},{448,704},{257,513},{321,577},{385,6... | collective-permute-start | bytes 24584 | tf_op jit(solution)/shard_map/chain/ppermute | solution.py:296
  22.7 0.0 collective-permute-done.2.come_ref.refs_0_
  22.7 0.7 %collective-permute-start.3 = (f32[16,128]{1,0:T(8,128)S(1)}, f32[16,128]{1,0:T(8,128)S(1)}, u32[]{:S(2)}, u32[]{:S(2)}) collective-permute-start(f32[16,128]{1,0:T(8,128)S(1)} %chain.3), channel_id=1, source_target_pairs={{512,768},{576,832},{640,896},{704,960},{513,769},{577,833},{641,8... | collective-permute-start | bytes 24584 | tf_op jit(solution)/shard_map/chain/ppermute | solution.py:296
  23.4 0.0 collective-permute-done.3.refs_1_
  23.4 0.4 gate.1
  23.8 18.1 %all_to_all.11.got_ref = f32[64,4,128]{2,1,0:T(4,128)S(1)} all-to-all(f32[64,4,128]{2,1,0:T(4,128)S(1)} %get-tuple-element.65), channel_id=1, replica_groups={{41,42,43,44,45,46,47,48,49,50,51,52,53,54,55,56,57,58,59,60,61,62,63,0..., dimensions={0} | all-to-all | bytes 262144 | tf_op jit(solution)/shard_map/exchange_squares/all_to_all | solution.py:309
  41.9 0.9 %normalize.1 = bf16[512,128]{1,0:T(8,128)(2,1)} custom-call(f32[64,4,128]{2,1,0:T(4,128)S(1)} %all_to_all.11.got_ref, f32[512,128]{1,0:T(8,128)S(1)} %get-tuple-element.66.out_ref), custom_call_target="tpu_custom_call" | custom-call | flops 1000000 | bytes 1000000 | tf_op jit(solution)/shard_map/normalize/pallas_call | solution.py:311
  (4 shorter events, 0.1 us)
Async XLA Ops:
  1.4 12.2 %collective-permute-start.1 = (f32[16,128]{1,0:T(8,128)S(1)}, f32[16,128]{1,0:T(8,128)S(1)}, u32[]{:S(2)}, u32[]{:S(2)}) collective-permute-start(f32[16,128]{1,0:T(8,128)S(1)} %get-tuple-element.36.own0_ref), channel_id=1, source_target_pairs={{0,256},{1,257},{2,258},{3,259},{4,260},{5,261},{6,262},{7,263},{8... | collective-permute-start | bytes 24584 | tf_op jit(solution)/shard_map/end_state/ppermute | solution.py:280
  11.5 2.0 %collective-permute-start = (f32[16,128]{1,0:T(8,128)S(1)}, f32[16,128]{1,0:T(8,128)S(1)}, u32[]{:S(2)}, u32[]{:S(2)}) collective-permute-start(f32[16,128]{1,0:T(8,128)S(1)} %get-tuple-element.36.own0_ref), channel_id=1, source_target_pairs={{64,256},{128,320},{192,384},{65,257},{129,321},{193,385},{66,258}... | collective-permute-start | bytes 24584 | tf_op jit(solution)/shard_map/end_state/ppermute | solution.py:281
  22.0 0.7 %collective-permute-start.2 = (f32[16,128]{1,0:T(8,128)S(1)}, f32[16,128]{1,0:T(8,128)S(1)}, u32[]{:S(2)}, u32[]{:S(2)}) collective-permute-start(f32[16,128]{1,0:T(8,128)S(1)} %get-tuple-element.48.after_ref.own_ref), channel_id=1, source_target_pairs={{256,512},{320,576},{384,640},{448,704},{257,513},{321,577},{385,6... | collective-permute-start | bytes 24584 | tf_op jit(solution)/shard_map/chain/ppermute | solution.py:296
  22.7 0.7 %collective-permute-start.3 = (f32[16,128]{1,0:T(8,128)S(1)}, f32[16,128]{1,0:T(8,128)S(1)}, u32[]{:S(2)}, u32[]{:S(2)}) collective-permute-start(f32[16,128]{1,0:T(8,128)S(1)} %chain.3), channel_id=1, source_target_pairs={{512,768},{576,832},{640,896},{704,960},{513,769},{577,833},{641,8... | collective-permute-start | bytes 24584 | tf_op jit(solution)/shard_map/chain/ppermute | solution.py:296

commit v6 on v4

--- a/solution.py
+++ b/solution.py
@@ -227,13 +227,15 @@
 
 
 def norm_kernel(got_ref, out_ref, mixed_ref):
-    width = out_ref.shape[1]
-    total = jnp.sum(got_ref[...], axis=0)
-    scale = lax.rsqrt(total / D + EPS)
+    parts = got_ref[...]
+    while parts.shape[0] > 1:
+        half = parts.shape[0] // 2
+        parts = parts[:half] + parts[half:]
+    scale = lax.rsqrt(parts[0] / D + EPS)
+    columns = jnp.transpose(jnp.concatenate([scale, scale], axis=0))
     for i in range(scale.shape[0]):
         part = pl.ds(i * CHUNK, CHUNK)
-        column = jnp.transpose(jnp.broadcast_to(scale[i : i + 1], (width, CHUNK)))
-        mixed_ref[part, :] = (out_ref[part, :] * column).astype(BF16)
+        mixed_ref[part, :] = (out_ref[part, :] * columns[:, i : i + 1]).astype(BF16)
 
 
 def call(kernel, outs, flops, size, **more):

time: 43 us -> 43 us (level)
  no operation moved by 1% of the time
where the time goes in v6:
time: 43 us; the launch traced here: 42.8 us
  blocking collectives  27.1 us (63%)
  starting transfers between devices  11.5 us (27%)
  Pallas kernels  4.11 us (10%)
    all_to_all x1, blocking collectives, local(): got = lax.all_to_all(send, 'chan', 0, 0, axis_index_groups=[order])  17 us
    ppermute x1, starting transfers between devices, local(): come = lax.ppermute(own0, 'ctx', [(i, RUN + i) for i in range(RUN)])  10.2 us
    all_to_all x1, blocking collectives, local(): got = lax.all_to_all(send, 'ctx', 0, 0, axis_index_groups=runs)  10.1 us
    pallas_call x2, Pallas kernels, ends(): call(functools.partial(kernel, n), (state_shape, state_shape, *(shape(x.s...  2.69 us
    ppermute x2, starting transfers between devices, local(): come.append(lax.ppermute(upto, 'ctx', links))  1.32 us
    pallas_call x1, Pallas kernels, local(): call(norm_kernel, shape((tokens, width), BF16), 10 ** 6, 10 ** 6)(got, out)  0.94 us
  transfers between devices with their start and end apart: 3, of which 0 were waited for; matrix products, arithmetic and copies ran while one was open for 0% of the time, Pallas kernels for 3%

profile of v6, /device:TPU:1, one launch (start us, length us, event | category | flops | bytes accessed | tf_op | source)
XLA Modules:
  0.0 42.8 jit_solution(16296125542579294893)
XLA Ops:
  0.0 1.3 %end_state.2 = (f32[16,128]{1,0:T(8,128)S(1)}, f32[16,128]{1,0:T(8,128)S(1)}, f32[8,16]{1,0:T(8,128)S(1)}, bf16[512,128]{1,0:T(8,128)(2,1)S(1)}, bf16[512,128]{1...) custom-call(f32[8,16]{1,0:T(8,128)} %refs_0_.3, ...), custom_call_target="tpu_custom_call" | custom-call | flops 100000000 | bytes 1000000 | tf_op jit(solution)/shard_map/end_state/pallas_call | solution.py:264
  1.4 10.2 %collective-permute-start = (f32[16,128]{1,0:T(8,128)S(1)}, f32[16,128]{1,0:T(8,128)S(1)}, u32[]{:S(2)}, u32[]{:S(2)}) collective-permute-start(f32[16,128]{1,0:T(8,128)S(1)} %get-tuple-element.36.own0_ref), channel_id=1, source_target_pairs={{0,256},{64,320},{128,384},{192,448},{1,257},{65,321},{129,385},{1... | collective-permute-start | bytes 24584 | tf_op jit(solution)/shard_map/end_state/ppermute | solution.py:278
  11.5 1.3 %end_state.3 = (f32[16,128]{1,0:T(8,128)S(1)}, f32[16,128]{1,0:T(8,128)S(1)}, f32[8,16]{1,0:T(8,128)S(1)}, bf16[512,128]{1,0:T(8,128)(2,1)S(1)}, bf16[512,128]{1...) custom-call(f32[8,16]{1,0:T(8,128)} %refs_0_.3, ...), custom_call_target="tpu_custom_call" | custom-call | flops 100000000 | bytes 1000000 | tf_op jit(solution)/shard_map/end_state/pallas_call | solution.py:264
  12.9 0.0 collective-permute-done.come_ref
  12.9 10.1 %all_to_all.10.got_ref = f32[4,32,128]{2,1,0:T(8,128)S(1)} all-to-all(f32[4,32,128]{2,1,0:T(8,128)S(1)} %get-tuple-element.45), channel_id=1, replica_groups={{192,128,64,0},{448,384,320,256},{704,640,576,512},{960,896,832,768},{1..., dimensions={0} | all-to-all | bytes 131072 | tf_op jit(solution)/shard_map/exchange_in_run/all_to_all | solution.py:285
  23.1 0.7 %collective-permute-start.1 = (f32[16,128]{1,0:T(8,128)S(1)}, f32[16,128]{1,0:T(8,128)S(1)}, u32[]{:S(2)}, u32[]{:S(2)}) collective-permute-start(f32[16,128]{1,0:T(8,128)S(1)} %get-tuple-element.48.after_ref.own_ref), channel_id=1, source_target_pairs={{256,512},{320,576},{384,640},{448,704},{257,513},{321,577},{385,6... | collective-permute-start | bytes 24584 | tf_op jit(solution)/shard_map/chain/ppermute | solution.py:293
  23.8 0.0 collective-permute-done.1.come_ref.refs_0_
  23.8 0.7 %collective-permute-start.2 = (f32[16,128]{1,0:T(8,128)S(1)}, f32[16,128]{1,0:T(8,128)S(1)}, u32[]{:S(2)}, u32[]{:S(2)}) collective-permute-start(f32[16,128]{1,0:T(8,128)S(1)} %chain.3), channel_id=1, source_target_pairs={{512,768},{576,832},{640,896},{704,960},{513,769},{577,833},{641,8... | collective-permute-start | bytes 24584 | tf_op jit(solution)/shard_map/chain/ppermute | solution.py:293
  24.5 0.0 collective-permute-done.2.refs_1_
  24.5 0.4 gate.1
  24.9 17.0 %all_to_all.11.got_ref = f32[64,4,128]{2,1,0:T(4,128)S(1)} all-to-all(f32[64,4,128]{2,1,0:T(4,128)S(1)} %get-tuple-element.65), channel_id=1, replica_groups={{41,42,43,44,45,46,47,48,49,50,51,52,53,54,55,56,57,58,59,60,61,62,63,0..., dimensions={0} | all-to-all | bytes 262144 | tf_op jit(solution)/shard_map/exchange_squares/all_to_all | solution.py:306
  41.9 0.9 %normalize.1 = bf16[512,128]{1,0:T(8,128)(2,1)} custom-call(f32[64,4,128]{2,1,0:T(4,128)S(1)} %all_to_all.11.got_ref, f32[512,128]{1,0:T(8,128)S(1)} %get-tuple-element.66.out_ref), custom_call_target="tpu_custom_call" | custom-call | flops 1000000 | bytes 1000000 | tf_op jit(solution)/shard_map/normalize/pallas_call | solution.py:308
  (4 shorter events, 0.1 us)
Async XLA Ops:
  1.4 11.5 %collective-permute-start = (f32[16,128]{1,0:T(8,128)S(1)}, f32[16,128]{1,0:T(8,128)S(1)}, u32[]{:S(2)}, u32[]{:S(2)}) collective-permute-start(f32[16,128]{1,0:T(8,128)S(1)} %get-tuple-element.36.own0_ref), channel_id=1, source_target_pairs={{0,256},{64,320},{128,384},{192,448},{1,257},{65,321},{129,385},{1... | collective-permute-start | bytes 24584 | tf_op jit(solution)/shard_map/end_state/ppermute | solution.py:278
  23.1 0.7 %collective-permute-start.1 = (f32[16,128]{1,0:T(8,128)S(1)}, f32[16,128]{1,0:T(8,128)S(1)}, u32[]{:S(2)}, u32[]{:S(2)}) collective-permute-start(f32[16,128]{1,0:T(8,128)S(1)} %get-tuple-element.48.after_ref.own_ref), channel_id=1, source_target_pairs={{256,512},{320,576},{384,640},{448,704},{257,513},{321,577},{385,6... | collective-permute-start | bytes 24584 | tf_op jit(solution)/shard_map/chain/ppermute | solution.py:293
  23.8 0.7 %collective-permute-start.2 = (f32[16,128]{1,0:T(8,128)S(1)}, f32[16,128]{1,0:T(8,128)S(1)}, u32[]{:S(2)}, u32[]{:S(2)}) collective-permute-start(f32[16,128]{1,0:T(8,128)S(1)} %chain.3), channel_id=1, source_target_pairs={{512,768},{576,832},{640,896},{704,960},{513,769},{577,833},{641,8... | collective-permute-start | bytes 24584 | tf_op jit(solution)/shard_map/chain/ppermute | solution.py:293
